TPU v7x, 32 devices: a whole 2x2x4 slice. The times are simulated.
32 devices in a mesh: ctx: 16 (over z, x, core), fsdp: 2 (over y).
Axes of the slice: x: 2, y: 2, z: 4, core: 2. Of those that a mesh axis runs over, the one named last changes fastest.
Arguments:
- hidden_in: bfloat16 [2, 2048, 1024], P('fsdp', 'ctx'), may hold values from -6 to 6
- doc_lengths: int32 [2, 8], P('fsdp'), may hold values from 1 to 1920, as said below
- attn_gain: float32 [1024], replicated, may hold values from 0.5 to 1.5
- query_gain: float32 [64], replicated, may hold values from 0.5 to 1.5
- key_norm_gain: float32 [64], replicated, may hold values from 0.5 to 1.5
- ffn_gain: float32 [1024], replicated, may hold values from 0.5 to 1.5
- query_proj: float32 [1024, 1024], P('fsdp'), may hold values from -0.1875 to 0.1875
- key_weight: float32 [1024, 512], P('fsdp'), may hold values from -0.1875 to 0.1875
- value_weight: float32 [1024, 512], P('fsdp'), may hold values from -0.1875 to 0.1875
- attn_proj: float32 [1024, 1024], P('fsdp'), may hold values from -3 to 3
- gate_proj: float32 [1024, 4608], P('fsdp'), may hold values from -0.1875 to 0.1875
- up_proj: float32 [1024, 4608], P('fsdp'), may hold values from -0.1875 to 0.1875
- down_proj: float32 [4608, 1024], P('fsdp'), may hold values from -0.09375 to 0.09375
- out_cotangent: bfloat16 [2, 2048, 1024], P('fsdp', 'ctx'), may hold values from -6 to 6
Outputs:
- hidden_out: float32 [2, 2048, 1024], P('fsdp', 'ctx')
- input_grad: float32 [2, 2048, 1024], P('fsdp', 'ctx')
- attn_gain_grad: float32 [1024], replicated
- query_gain_grad: float32 [64], replicated
- key_gain_grad: float32 [64], replicated
- ffn_gain_grad: float32 [1024], replicated
- query_grad: float32 [1024, 1024], P('fsdp', 'ctx')
- key_grad: float32 [1024, 512], P('fsdp', 'ctx')
- value_grad: float32 [1024, 512], P('fsdp', 'ctx')
- attn_grad: float32 [1024, 1024], P('fsdp', 'ctx')
- gate_grad: float32 [1024, 4608], P('fsdp', 'ctx')
- up_grad: float32 [1024, 4608], P('fsdp', 'ctx')
- down_grad: float32 [4608, 1024], P('fsdp', 'ctx')
Inputs may be any that keep to these rules, and one draw needn't show every extreme that they name: `doc_lengths`: each stream's 8 document lengths sum to 2048; in every stream exactly one document has 1920 tokens, and it is neither the first nor the last of its stream.
All inputs are finite; a program needn't handle non-finite values.
Results may differ from a plain program's by a relative error of at most 0.014.
Values may be sent and summed in bfloat16 or wider, within the bound.
A program may use at most 320 MiB of HBM per device.

v0:
```python
import jax
import jax.numpy as jnp
from jax import lax
from jax.sharding import PartitionSpec as P

QUERY_HEADS = 16
KEY_VALUE_HEADS = 8
HEAD_SIZE = 64
FF = 4608


epsilon = 1e-05
rope_base = 1000000.0


def root_mean_norm(value_rows, gain):
    return (
        value_rows
        * lax.rsqrt(jnp.mean(value_rows * value_rows, axis=-1, keepdims=True) + epsilon)
        * gain
    )


def apply_rotary(value_rows, token_positions):
    halfway = value_rows.shape[-1] // 2
    freqs = rope_base ** (-2.0 * jnp.arange(halfway, dtype=jnp.float32) / value_rows.shape[-1])
    angles = token_positions.astype(jnp.float32)[:, None] * freqs[None, :]
    cosine = jnp.cos(angles)[:, None, :]
    sine_part = jnp.sin(angles)[:, None, :]
    leading = value_rows[..., :halfway]
    trailing = value_rows[..., halfway:]
    return jnp.concatenate(
        [leading * cosine - trailing * sine_part, leading * sine_part + trailing * cosine], axis=-1
    )


def locate(token_index, starts):
    after = token_index[:, None] >= starts[None, :]
    document_index = jnp.sum(after.astype(jnp.int32), axis=1)
    begins = jnp.max(jnp.where(after, starts[None, :], 0), axis=1)
    return (document_index, token_index - begins)


def swiglu(gate_in, up_in):
    return jax.nn.silu(gate_in) * up_in


def block_size(length):
    segment_length = length
    while segment_length > 1024 and segment_length % 2 == 0:
        segment_length = segment_length // 2
    return segment_length


def lead_sum(left, right):
    return lax.dot_general(
        left, right, (((0,), (0,)), ((), ())), preferred_element_type=jnp.float32
    )


def back_product(left, right):
    return lax.dot_general(
        left, right, (((1,), (1,)), ((), ())), preferred_element_type=jnp.float32
    )


def forward_product(left, right):
    return jnp.dot(left, right, preferred_element_type=jnp.float32)


def allowed_pairs(query_doc, query_index, key_doc, key_index):
    return (query_doc[:, None] == key_doc[None, :]) & (query_index[:, None] >= key_index[None, :])


def exp_scores(query_group, key_block, allowed):
    scores = jnp.einsum(
        "qgrd,kgd->qgrk", query_group, key_block, preferred_element_type=jnp.float32
    )
    return jnp.where(allowed[:, None, None, :], jnp.exp(scores), 0.0)


def arrange_blocks(term, cycle_count, pair_count):
    height, width = term.shape
    shaped = term.reshape(pair_count, height // pair_count, cycle_count, width // cycle_count)
    return jnp.transpose(shaped, (2, 0, 1, 3)).reshape(cycle_count * height, width // cycle_count)


def local(
    hidden_in,
    doc_lengths,
    attn_gain,
    query_gain,
    key_norm_gain,
    ffn_gain,
    query_proj,
    key_weight,
    value_weight,
    attn_proj,
    gate_proj,
    up_proj,
    down_proj,
    out_cotangent,
):
    token_rows = hidden_in.shape[1]
    query_per_key = QUERY_HEADS // KEY_VALUE_HEADS
    query_width = QUERY_HEADS * HEAD_SIZE
    key_total_width = KEY_VALUE_HEADS * HEAD_SIZE
    token_index = lax.axis_index("ctx") * token_rows + jnp.arange(token_rows, dtype=jnp.int32)
    lengths = doc_lengths[0]
    starts = jnp.cumsum(lengths) - lengths
    document_index, token_positions = locate(token_index, starts)
    stacked_proj = jnp.concatenate(
        [
            query_proj.astype(jnp.bfloat16),
            key_weight.astype(jnp.bfloat16),
            value_weight.astype(jnp.bfloat16),
        ],
        axis=1,
    )
    output_local = attn_proj.astype(jnp.bfloat16)
    glu_local = jnp.concatenate(
        [gate_proj.astype(jnp.bfloat16), up_proj.astype(jnp.bfloat16)], axis=1
    )
    down_local = down_proj.astype(jnp.bfloat16)
    w_stacked, w_output, w_glu, w_down = (
        lax.all_gather(stacked_proj, "fsdp", axis=0, tiled=True),
        lax.all_gather(output_local, "fsdp", axis=0, tiled=True),
        lax.all_gather(glu_local, "fsdp", axis=0, tiled=True),
        lax.all_gather(down_local, "fsdp", axis=0, tiled=True),
    )

    def project_in(inputs, weight):
        return (forward_product(inputs, weight), inputs)

    def project_back(grads, weight):
        return (back_product(grads, weight), grads)

    resid = hidden_in[0].astype(jnp.float32)
    normed_full, attn_back = jax.vjp(root_mean_norm, resid, attn_gain)
    normed = normed_full.astype(jnp.bfloat16)
    stacked_out, normed_side = project_in(normed, w_stacked)
    query_pre = stacked_out[:, :query_width]
    key_before_norm = stacked_out[:, query_width : query_width + key_total_width]
    value_rows_narrow = stacked_out[:, query_width + key_total_width :].astype(jnp.bfloat16)

    def rotate_heads(query_in, key_input, query_scale, key_norm_scale):
        query_rotated = apply_rotary(
            root_mean_norm(query_in.reshape(token_rows, QUERY_HEADS, HEAD_SIZE), query_scale),
            token_positions,
        ) * HEAD_SIZE ** (-0.5)
        key_rotated = apply_rotary(
            root_mean_norm(
                key_input.reshape(token_rows, KEY_VALUE_HEADS, HEAD_SIZE), key_norm_scale
            ),
            token_positions,
        )
        return (query_rotated, key_rotated)

    (query_rotated, key_rotated), heads_back = jax.vjp(
        rotate_heads, query_pre, key_before_norm, query_gain, key_norm_gain
    )
    query_rows = query_rotated.reshape(
        token_rows, KEY_VALUE_HEADS, query_per_key, HEAD_SIZE
    ).astype(jnp.bfloat16)
    key_rows_narrow = key_rotated.reshape(token_rows, KEY_VALUE_HEADS * HEAD_SIZE).astype(
        jnp.bfloat16
    )
    start_state = (
        jnp.zeros((token_rows, KEY_VALUE_HEADS, query_per_key, HEAD_SIZE), jnp.float32),
        jnp.zeros((token_rows, KEY_VALUE_HEADS, query_per_key), jnp.float32),
    )
    key_segment = lax.all_gather(key_rows_narrow, "ctx", axis=0, tiled=True)
    value_segment = lax.all_gather(value_rows_narrow, "ctx", axis=0, tiled=True)
    segment_length = block_size(key_segment.shape[0])
    block_count = key_segment.shape[0] // segment_length
    key_segments = key_segment.reshape(block_count, segment_length, KEY_VALUE_HEADS, HEAD_SIZE)
    value_segments = value_segment.reshape(block_count, segment_length, KEY_VALUE_HEADS, HEAD_SIZE)
    offsets = segment_length * jnp.arange(block_count, dtype=jnp.int32)

    def forward_step(inner, item):
        key_block, value_block, offset = item
        key_index = offset + jnp.arange(segment_length, dtype=jnp.int32)
        allowed = allowed_pairs(
            document_index, token_index, locate(key_index, starts)[0], key_index
        )
        weights = exp_scores(query_rows, key_block, allowed)
        summed_next = inner[0] + jnp.einsum(
            "qgrk,kgd->qgrd",
            weights.astype(jnp.bfloat16),
            value_block,
            preferred_element_type=jnp.float32,
        )
        return ((summed_next, inner[1] + jnp.sum(weights, axis=-1)), None)

    summed, totals = lax.scan(forward_step, start_state, (key_segments, value_segments, offsets))[0]
    mixed_heads = (summed / totals[..., None]).reshape(token_rows, QUERY_HEADS * HEAD_SIZE)
    attended = mixed_heads.astype(jnp.bfloat16)
    attn_out, attended_side = project_in(attended, w_output)
    middle = resid + attn_out
    ffn_full, ffn_back = jax.vjp(root_mean_norm, middle, ffn_gain)
    normed_ffn = ffn_full.astype(jnp.bfloat16)
    glu_out, ffn_side = project_in(normed_ffn, w_glu)
    gate = glu_out[:, :FF]
    up_part = glu_out[:, FF:]
    hidden_full, glu_back = jax.vjp(swiglu, gate, up_part)
    hidden = hidden_full.astype(jnp.bfloat16)
    down_out, hidden_side = project_in(hidden, w_down)
    output = middle + down_out
    cotangent = out_cotangent[0]
    grad_hidden, cotangent_side = project_back(cotangent, w_down)
    down_term = lead_sum(hidden_side, cotangent_side)
    grad_gate, grad_up = glu_back(grad_hidden)
    glu_low = jnp.concatenate(
        [grad_gate.astype(jnp.bfloat16), grad_up.astype(jnp.bfloat16)], axis=1
    )
    grad_ffn_in, glu_side = project_back(glu_low, w_glu)
    glu_term = lead_sum(ffn_side, glu_side)
    gate_term = glu_term[:, :FF]
    up_term = glu_term[:, FF:]
    grad_mid_norm, ffn_gain_part = ffn_back(grad_ffn_in)
    grad_middle = cotangent.astype(jnp.float32) + grad_mid_norm
    branch_low = grad_middle.astype(jnp.bfloat16)
    mixed_gradient_flat, branch_side = project_back(branch_low, w_output)
    attn_term = lead_sum(attended_side, branch_side)
    mixed_gradient = mixed_gradient_flat.reshape(
        token_rows, KEY_VALUE_HEADS, query_per_key, HEAD_SIZE
    )
    grad_summed = (mixed_gradient / totals[..., None]).astype(jnp.bfloat16)
    deltas = jnp.sum(mixed_gradient * summed, axis=-1) / (totals * totals)
    key_segment = lax.all_gather(key_rows_narrow, "ctx", axis=0, tiled=True)
    value_segment = lax.all_gather(value_rows_narrow, "ctx", axis=0, tiled=True)
    query_segment_length = block_size(key_segment.shape[0])
    block_count = key_segment.shape[0] // query_segment_length
    key_segments = key_segment.reshape(
        block_count, query_segment_length, KEY_VALUE_HEADS, HEAD_SIZE
    )
    value_segments = value_segment.reshape(
        block_count, query_segment_length, KEY_VALUE_HEADS, HEAD_SIZE
    )
    offsets = query_segment_length * jnp.arange(block_count, dtype=jnp.int32)

    def query_step(inner, item):
        key_block, value_block, offset = item
        key_index = offset + jnp.arange(query_segment_length, dtype=jnp.int32)
        allowed = allowed_pairs(
            document_index, token_index, locate(key_index, starts)[0], key_index
        )
        weights = exp_scores(query_rows, key_block, allowed)
        grad_prob = jnp.einsum(
            "qgrd,kgd->qgrk", grad_summed, value_block, preferred_element_type=jnp.float32
        )
        grad_scores = (weights * (grad_prob - deltas[..., None])).astype(jnp.bfloat16)
        return (
            inner
            + jnp.einsum(
                "qgrk,kgd->qgrd", grad_scores, key_block, preferred_element_type=jnp.float32
            ),
            None,
        )

    grad_queries = lax.scan(
        query_step,
        jnp.zeros((token_rows, KEY_VALUE_HEADS, query_per_key, HEAD_SIZE), jnp.float32),
        (key_segments, value_segments, offsets),
    )[0]
    key_rows_local = key_rows_narrow.reshape(token_rows, KEY_VALUE_HEADS, HEAD_SIZE)
    value_rows_local = value_rows_narrow.reshape(token_rows, KEY_VALUE_HEADS, HEAD_SIZE)
    key_offset = (
        jnp.zeros((token_rows, KEY_VALUE_HEADS, HEAD_SIZE), jnp.float32),
        jnp.zeros((token_rows, KEY_VALUE_HEADS, HEAD_SIZE), jnp.float32),
    )
    query_segment = lax.all_gather(
        query_rows.reshape(token_rows, QUERY_HEADS * HEAD_SIZE), "ctx", axis=0, tiled=True
    )
    gradient_segment = lax.all_gather(
        grad_summed.reshape(token_rows, QUERY_HEADS * HEAD_SIZE), "ctx", axis=0, tiled=True
    )
    delta_segment = lax.all_gather(
        deltas.reshape(token_rows, QUERY_HEADS).astype(jnp.bfloat16), "ctx", axis=0, tiled=True
    ).astype(jnp.float32)
    key_segment_length = block_size(query_segment.shape[0])
    block_count = query_segment.shape[0] // key_segment_length
    query_segments = query_segment.reshape(
        block_count, key_segment_length, KEY_VALUE_HEADS, query_per_key, HEAD_SIZE
    )
    gradient_blocks = gradient_segment.reshape(
        block_count, key_segment_length, KEY_VALUE_HEADS, query_per_key, HEAD_SIZE
    )
    delta_rows_all = delta_segment.reshape(
        block_count, key_segment_length, KEY_VALUE_HEADS, query_per_key
    )
    offsets = key_segment_length * jnp.arange(block_count, dtype=jnp.int32)

    def key_step(inner, item):
        query_block, grad_block, delta_block, offset = item
        query_index = offset + jnp.arange(key_segment_length, dtype=jnp.int32)
        allowed = allowed_pairs(
            locate(query_index, starts)[0], query_index, document_index, token_index
        )
        weights = exp_scores(query_block, key_rows_local, allowed)
        grad_prob = jnp.einsum(
            "qgrd,kgd->qgrk", grad_block, value_rows_local, preferred_element_type=jnp.float32
        )
        grad_scores = (weights * (grad_prob - delta_block[..., None])).astype(jnp.bfloat16)
        key_next = inner[0] + jnp.einsum(
            "qgrk,qgrd->kgd", grad_scores, query_block, preferred_element_type=jnp.float32
        )
        value_next = inner[1] + jnp.einsum(
            "qgrk,qgrd->kgd",
            weights.astype(jnp.bfloat16),
            grad_block,
            preferred_element_type=jnp.float32,
        )
        return ((key_next, value_next), None)

    grad_keys, value_gradients = lax.scan(
        key_step, key_offset, (query_segments, gradient_blocks, delta_rows_all, offsets)
    )[0]
    grad_query_pre, grad_key_pre, query_gain_part, key_gain_part = heads_back(
        (grad_queries.reshape(token_rows, QUERY_HEADS, HEAD_SIZE), grad_keys)
    )
    stacked_low = jnp.concatenate(
        [
            grad_query_pre.astype(jnp.bfloat16),
            grad_key_pre.astype(jnp.bfloat16),
            value_gradients.reshape(token_rows, KEY_VALUE_HEADS * HEAD_SIZE).astype(jnp.bfloat16),
        ],
        axis=1,
    )
    grad_normed, stacked_side = project_back(stacked_low, w_stacked)
    stacked_term = lead_sum(normed_side, stacked_side)
    query_term = stacked_term[:, :query_width]
    key_term = stacked_term[:, query_width : query_width + key_total_width]
    value_term = stacked_term[:, query_width + key_total_width :]
    grad_resid, attn_gain_part = attn_back(grad_normed)
    input_grad = grad_middle + grad_resid
    cycle_count = lax.axis_size("ctx")
    pair_count = lax.axis_size("fsdp")
    shares = (
        lax.psum_scatter(
            arrange_blocks(query_term, cycle_count, pair_count),
            ("ctx", "fsdp"),
            scatter_dimension=0,
            tiled=True,
        ),
        lax.psum_scatter(
            arrange_blocks(key_term, cycle_count, pair_count),
            ("ctx", "fsdp"),
            scatter_dimension=0,
            tiled=True,
        ),
        lax.psum_scatter(
            arrange_blocks(value_term, cycle_count, pair_count),
            ("ctx", "fsdp"),
            scatter_dimension=0,
            tiled=True,
        ),
        lax.psum_scatter(
            arrange_blocks(attn_term, cycle_count, pair_count),
            ("ctx", "fsdp"),
            scatter_dimension=0,
            tiled=True,
        ),
        lax.psum_scatter(
            arrange_blocks(gate_term, cycle_count, pair_count),
            ("ctx", "fsdp"),
            scatter_dimension=0,
            tiled=True,
        ),
        lax.psum_scatter(
            arrange_blocks(up_term, cycle_count, pair_count),
            ("ctx", "fsdp"),
            scatter_dimension=0,
            tiled=True,
        ),
        lax.psum_scatter(
            arrange_blocks(down_term, cycle_count, pair_count),
            ("ctx", "fsdp"),
            scatter_dimension=0,
            tiled=True,
        ),
    )
    gain_grads = lax.psum(
        (attn_gain_part, query_gain_part, key_gain_part, ffn_gain_part), ("ctx", "fsdp")
    )
    return (
        output[None],
        input_grad[None],
        gain_grads[0],
        gain_grads[1],
        gain_grads[2],
        gain_grads[3],
        shares[0],
        shares[1],
        shares[2],
        shares[3],
        shares[4],
        shares[5],
        shares[6],
    )


def solution(mesh):
    in_specs = (
        P("fsdp", "ctx", None),
        P("fsdp", None),
        P(),
        P(),
        P(),
        P(),
        P("fsdp", None),
        P("fsdp", None),
        P("fsdp", None),
        P("fsdp", None),
        P("fsdp", None),
        P("fsdp", None),
        P("fsdp", None),
        P("fsdp", "ctx", None),
    )
    out_specs = (
        P("fsdp", "ctx", None),
        P("fsdp", "ctx", None),
        P(),
        P(),
        P(),
        P(),
        P("fsdp", "ctx"),
        P("fsdp", "ctx"),
        P("fsdp", "ctx"),
        P("fsdp", "ctx"),
        P("fsdp", "ctx"),
        P("fsdp", "ctx"),
        P("fsdp", "ctx"),
    )
    return jax.shard_map(local, mesh=mesh, in_specs=in_specs, out_specs=out_specs, check_vma=False)
```

profile of v0, /device:TPU:0, one launch (start us, length us, event | category | flops | bytes accessed | tf_op | source)
XLA Modules:
  0.0 1839.4 jit_solution(13888813296637231658)
XLA Ops:
  12.5 58.9 %all-gather.9.cloned.1.call-done = bf16[1024,2048]{1,0:T(8,128)(2,1)} async-done(((bf16[512,2048]{1,0:T(8,128)(2,1)}), bf16[1024,2048]{1,0:T(8,128)(2,1)}) %all-gather.9.cloned.1.call-update) | async-done | bytes 4194320 | tf_op jit(solution)/shard_map/all_gather | solution.py:126
  92.5 6.6 convert_element_type.150
  100.9 17.6 all-gather.13.cloned.1.call-done
  125.2 36.3 %all-gather.11.cloned.1.call-done = bf16[2048,512]{1,0:T(8,128)(2,1)} async-done(((bf16[128,512]{1,0:T(8,128)(2,1)}), bf16[2048,512]{1,0:T(8,128)(2,1)}) %all-gather.11.cloned.1.call-update) | async-done | bytes 2097168 | tf_op jit(solution)/shard_map/all_gather | solution.py:173
  161.6 6.2 reshape.489
  167.8 5.7 copy.119
  173.5 10.1 while.37
  187.3 7.6 all-gather.15.cloned.1.call-done
  197.8 222.9 %all-gather.17.cloned.1.call-done = bf16[1024,9216]{1,0:T(8,128)(2,1)} async-done(((bf16[512,9216]{1,0:T(8,128)(2,1)}), bf16[1024,9216]{1,0:T(8,128)(2,1)}) %all-gather.17.cloned.1.call-update) | async-done | bytes 18874384 | tf_op jit(solution)/shard_map/all_gather | solution.py:128
  420.7 11.9 fusion.141
  432.7 107.5 %all-gather.19.cloned.1.call-done = bf16[4608,1024]{1,0:T(8,128)(2,1)} async-done(((bf16[2304,1024]{1,0:T(8,128)(2,1)}), bf16[4608,1024]{1,0:T(8,128)(2,1)}) %all-gather.19.cloned.1.call-update) | async-done | bytes 9437200 | tf_op jit(solution)/shard_map/all_gather | solution.py:129
  540.2 10.0 fusion.104
  550.2 12.0 multiply_reduce_fusion
  566.4 29.8 %all-gather.21.cloned.1.call-done = bf16[2048,1024]{0,1:T(8,128)(2,1)} async-done(((bf16[128,1024]{0,1:T(8,128)(2,1)}), bf16[2048,1024]{0,1:T(8,128)(2,1)}) %all-gather.21.cloned.1.call-update) | async-done | bytes 4194320 | tf_op jit(solution)/shard_map/all_gather | solution.py:272
  596.1 8.2 reshape.456
  620.8 6.6 reshape.467
  630.2 27.3 %while.38 = (s32[]{:T(128)}, f32[128,8,2,64]{0,3,2,1:T(8,128)}, bf16[2,1024,8,64]{1,3,2,0:T(8,128)(2,1)S(1)}, s32[128]{0:T(128)S(1)}, s32[2]{0:T(128)S(1)}, /*in...) while((s32[]{:T(128)}, f32[128,8,2,64]{0,3,2,1:T(8,128)}, ...), condition=%wide.region_15.16_spmd.clone, body=%wide.region_13.15_spmd.clone.sunk | while | flops 814375040 | bytes 21789892 | solution.py:261
  636.5 7.4 fusion.198
  650.2 7.4 fusion.198
  657.6 18.8 %all_gather.37 = bf16[2048,16]{0,1:T(8,128)(2,1)S(1)} all-gather(bf16[128,16]{0,1:T(8,128)(2,1)S(1)} %bitcast.369), channel_id=1, replica_groups=mesh['ctx'=16,'fsdp'=2] {'ctx'}, dimensions={0}, use_global_device_ids=true | all-gather | bytes 69632 | tf_op jit(solution)/shard_map/all_gather | solution.py:278
  678.7 16.1 reshape.488
  694.8 20.2 %copy.128 = bf16[2,1024,8,2,64]{1,4,3,2,0:T(8,128)(2,1)} copy(bf16[2,1024,8,2,64]{4,3,2,1,0:T(2,128)(2,1)} %reshape.488) | data formatting | bytes 8388608
  715.1 44.6 %while.39 = (s32[]{:T(128)}, f32[128,8,64]{0,2,1:T(8,128)S(1)}, f32[128,8,64]{0,2,1:T(8,128)S(1)}, bf16[2,1024,8,2,64]{1,4,3,2,0:T(8,128)(2,1)}, s32[2]{0:T(128)...) while((s32[]{:T(128)}, f32[128,8,64]{0,2,1:T(8,128)S(1)}, ...), condition=%wide.region_19.20_spmd.clone, body=%wide.region_17.19_spmd.clone.sunk | while | flops 1087004800 | bytes 35609812 | solution.py:316
  716.9 6.3 fusion.206
  723.2 8.4 fusion.207
  739.2 6.3 fusion.206
  745.5 8.5 fusion.207
  798.1 6.7 reshape.461
  804.8 6.6 copy.131
  811.4 6.6 reshape.462
  822.7 22.6 %copy.144 = f32[16,2,2304,64]{2,1,0,3:T(2,128)} copy(f32[16,2,2304,64]{2,3,0,1:T(8,128)S(1)} %convolution_bitcast_fusion) | data formatting | bytes 37748736 | tf_op jit(solution)/shard_map/transpose | solution.py:85
  845.4 20.5 %reshape.472 = f32[73728,64]{0,1:T(8,128)} reshape(f32[16,2,2304,64]{2,1,0,3:T(2,128)} %copy.144) | data formatting | bytes 37748736 | tf_op jit(solution)/shard_map/reshape | solution.py:85
  867.7 15.1 fusion.106
  882.8 26.5 %fusion.144 = (f32[1024,4608]{1,0:T(8,128)}, f32[1024,4608]{1,0:T(8,128)}) fusion(f32[1024,9216]{1,0:T(8,128)} %fusion.106), kind=kLoop, calls=%fused_computation.193 | loop fusion | bytes 75497472 | tf_op jit(solution)/shard_map/slice | solution.py:219
  909.3 18.7 %copy.140 = f32[1024,4608]{0,1:T(8,128)} copy(f32[1024,4608]{1,0:T(8,128)} %get-tuple-element.526) | data formatting | bytes 37748736 | tf_op jit(solution)/shard_map/slice | solution.py:219
  927.9 24.6 %reshape.470 = f32[2,512,16,288]{1,0,3,2:T(2,128)} reshape(f32[1024,4608]{0,1:T(8,128)} %copy.140) | data formatting | bytes 37748736 | tf_op jit(solution)/shard_map/reshape | solution.py:84
  952.5 13.5 copy.141
  966.0 24.7 %reshape.471 = f32[16384,288]{0,1:T(8,128)} reshape(f32[16,2,512,288]{2,1,0,3:T(2,128)} %copy.141) | data formatting | bytes 37748736 | tf_op jit(solution)/shard_map/reshape | solution.py:85
  990.8 18.7 %copy.138 = f32[1024,4608]{0,1:T(8,128)} copy(f32[1024,4608]{1,0:T(8,128)} %get-tuple-element.527) | data formatting | bytes 37748736 | tf_op jit(solution)/shard_map/slice | solution.py:218
  1009.6 24.7 %reshape.468 = f32[2,512,16,288]{1,0,3,2:T(2,128)} reshape(f32[1024,4608]{0,1:T(8,128)} %copy.138) | data formatting | bytes 37748736 | tf_op jit(solution)/shard_map/reshape | solution.py:84
  1034.2 13.5 copy.139
  1047.7 24.7 %reshape.469 = f32[16384,288]{0,1:T(8,128)} reshape(f32[16,2,512,288]{2,1,0,3:T(2,128)} %copy.139) | data formatting | bytes 37748736 | tf_op jit(solution)/shard_map/reshape | solution.py:85
  1073.8 6.1 fusion.108
  1081.6 38.0 %all-reduce.4 = (f32[1024]{0:T(1024)}, f32[64]{0:T(128)}, f32[64]{0:T(128)}, f32[1024]{0:T(1024)}) all-reduce(f32[1024]{0:T(1024)S(1)} %get-tuple-element.442, f32[64]{0:T(128)S(1)} %copy-done.66, f32[64]{0:T(128)S(1)} %copy-done.67, f32[1024]{0:T(1024)S(1)} %copy-done.65), channel_id=1, replica_groups=mesh['ctx'=16,'fsdp'=2] {'ctx','fsdp'}, use_global_device_ids=true, to_apply=%region_23.24 | all-reduce | flops 2176 | bytes 17408 | tf_op jit(solution)/shard_map/psum | solution.py:383
  1120.6 81.8 %reduce-scatter.8.cloned.1.call-done = f32[512,64]{0,1:T(8,128)} async-done(((f32[16384,64]{0,1:T(8,128)}), f32[512,64]{0,1:T(8,128)}) %reduce-scatter.8.cloned.1.call-update) | async-done | bytes 131088 | tf_op jit(solution)/shard_map/reduce_scatter | solution.py:340
  1202.4 209.0 %reduce-scatter.20.cloned.1.call-done = f32[2304,64]{0,1:T(8,128)} async-done(((f32[73728,64]{0,1:T(8,128)}), f32[2304,64]{0,1:T(8,128)}) %reduce-scatter.20.cloned.1.call-update) | async-done | bytes 589840 | tf_op jit(solution)/shard_map/reduce_scatter | solution.py:376
  1411.4 210.6 %reduce-scatter.18.cloned.1.call-done = f32[512,288]{0,1:T(8,128)} async-done(((f32[16384,288]{0,1:T(8,128)}), f32[512,288]{0,1:T(8,128)}) %reduce-scatter.18.cloned.1.call-update) | async-done | bytes 589840 | tf_op jit(solution)/shard_map/reduce_scatter | solution.py:370
  1622.0 210.6 %reduce-scatter.16.cloned.1.call-done = f32[512,288]{0,1:T(8,128)} async-done(((f32[16384,288]{0,1:T(8,128)}), f32[512,288]{0,1:T(8,128)}) %reduce-scatter.16.cloned.1.call-update) | async-done | bytes 589840 | tf_op jit(solution)/shard_map/reduce_scatter | solution.py:364
  (317 shorter events, 152.5 us)
Async XLA Ops:
  7.2 64.2 %all-gather.9.cloned.1.call-start = ((), (), s32[]{:S(2)}) async-start(), calls=%async_computation.7 | async-start | bytes 6291456 | tf_op jit(solution)/shard_map/all_gather | solution.py:126
  10.0 61.4 %copy-start.42 = (f32[1024]{0:T(1024)S(1)}, f32[1024]{0:T(1024)}, u32[]{:S(2)}) copy-start(f32[1024]{0:T(1024)} %param.22) | copy-start | bytes 12292
  11.8 64.5 %copy-start.63 = (f32[64]{0:T(128)S(1)}, f32[64]{0:T(128)}, u32[]{:S(2)}) copy-start(f32[64]{0:T(128)} %param.24) | copy-start | bytes 772
  11.8 106.7 %all-gather.13.cloned.1.call-start = ((), (), s32[]{:S(2)}) async-start(), calls=%async_computation.9 | async-start | bytes 2228224 | tf_op jit(solution)/shard_map/all_gather | solution.py:172
  12.3 65.5 %copy-start.68 = (f32[128]{0:T(128)}, f32[128]{0:T(128)S(1)}, u32[]{:S(2)}) copy-start(f32[128]{0:T(128)S(1)} %fusion.117) | copy-start | bytes 1540
  12.3 62.8 %copy-start.58 = (f32[128]{0:T(128)}, f32[128]{0:T(128)S(1)}, u32[]{:S(2)}) copy-start(f32[128]{0:T(128)S(1)} %fusion.135) | copy-start | bytes 1540
  12.5 87.5 %copy-start.36 = (f32[128,32]{0,1:T(8,128)}, f32[128,32]{0,1:T(8,128)S(1)}, u32[]{:S(2)}) copy-start(f32[128,32]{0,1:T(8,128)S(1)} %get-tuple-element.541) | copy-start | bytes 49156
  12.5 87.5 %copy-start.38 = (f32[128,32]{0,1:T(8,128)}, f32[128,32]{0,1:T(8,128)S(1)}, u32[]{:S(2)}) copy-start(f32[128,32]{0,1:T(8,128)S(1)} %get-tuple-element.542) | copy-start | bytes 49156
  12.5 65.4 %copy-start.20 = (f32[512,1024]{1,0:T(8,128)S(1)}, f32[512,1024]{1,0:T(8,128)}, u32[]{:S(2)}) copy-start(f32[512,1024]{1,0:T(8,128)} %param.29) | copy-start | bytes 6291460
  77.1 84.5 %all-gather.11.cloned.1.call-start = ((), (), s32[]{:S(2)}) async-start(), calls=%async_computation.8 | async-start | bytes 2228224 | tf_op jit(solution)/shard_map/all_gather | solution.py:173
  77.9 117.0 %all-gather.15.cloned.1.call-start = ((), (), s32[]{:S(2)}) async-start(), calls=%async_computation.10 | async-start | bytes 3145728 | tf_op jit(solution)/shard_map/all_gather | solution.py:127
  79.1 341.6 %all-gather.17.cloned.1.call-start = ((), (), s32[]{:S(2)}) async-start(), calls=%async_computation.11 | async-start | bytes 28311552 | tf_op jit(solution)/shard_map/all_gather | solution.py:128
  92.5 447.7 %all-gather.19.cloned.1.call-start = ((), (), s32[]{:S(2)}) async-start(), calls=%async_computation.12 | async-start | bytes 14155776 | tf_op jit(solution)/shard_map/all_gather | solution.py:129
  99.2 496.9 %all-gather.21.cloned.1.call-start = ((), (), s32[]{:S(2)}) async-start(), calls=%async_computation.13 | async-start | bytes 4456448 | tf_op jit(solution)/shard_map/all_gather | solution.py:272
  99.6 25.6 %copy-start.50 = (f32[128,16]{0,1:T(8,128)}, f32[128,16]{0,1:T(8,128)S(1)}, u32[]{:S(2)}) copy-start(f32[128,16]{0,1:T(8,128)S(1)} %multiply_reduce_fusion.6) | copy-start | bytes 24580
  99.8 25.4 %copy-start.45 = (f32[128,16]{0,1:T(8,128)}, f32[128,16]{0,1:T(8,128)S(1)}, u32[]{:S(2)}) copy-start(f32[128,16]{0,1:T(8,128)S(1)} %fusion.130) | copy-start | bytes 24580
  100.8 577.8 %all-gather.23.cloned.1.call-start = ((), (), s32[]{:S(2)}) async-start(), calls=%async_computation.14 | async-start | bytes 4456448 | tf_op jit(solution)/shard_map/all_gather | solution.py:275
  183.6 249.1 %copy-start.48 = (s32[8]{0:T(128)}, s32[8]{0:T(128)S(1)}, u32[]{:S(2)}) copy-start(s32[8]{0:T(128)S(1)} %get-tuple-element.931) | copy-start | bytes 100
  183.6 249.1 %copy-start.73 = (s32[2]{0:T(128)}, s32[2]{0:T(128)S(1)}, u32[]{:S(2)}) copy-start(s32[2]{0:T(128)S(1)} %get-tuple-element.940) | copy-start | bytes 28
  183.6 237.1 %copy-start.30 = (f32[1024]{0:T(1024)S(1)}, f32[1024]{0:T(1024)}, u32[]{:S(2)}) copy-start(f32[1024]{0:T(1024)} %param.25) | copy-start | bytes 12292
  197.8 234.8 %copy-start.70 = (f32[128]{0:T(128)}, f32[128]{0:T(128)S(1)}, u32[]{:S(2)}) copy-start(f32[128]{0:T(128)S(1)} %get-tuple-element.543) | copy-start | bytes 1540
  197.8 352.3 %copy-start.56 = (f32[128]{0:T(128)}, f32[128]{0:T(128)S(1)}, u32[]{:S(2)}) copy-start(f32[128]{0:T(128)S(1)} %fusion.136) | copy-start | bytes 1540
  565.5 555.1 %reduce-scatter.14.cloned.1.call-start = ((), (), s32[]{:S(2)}) async-start(), calls=%async_computation.18 | async-start | bytes 4325376 | tf_op jit(solution)/shard_map/reduce_scatter | solution.py:358
  629.3 491.3 %reduce-scatter.12.cloned.1.call-start = ((), (), s32[]{:S(2)}) async-start(), calls=%async_computation.17 | async-start | bytes 2162688 | tf_op jit(solution)/shard_map/reduce_scatter | solution.py:352
  630.2 47.4 %copy-start.37 = (f32[128,32]{0,1:T(8,128)S(1)}, f32[128,32]{0,1:T(8,128)}, u32[]{:S(2)}) copy-start(f32[128,32]{0,1:T(8,128)} %copy-done.36) | copy-start | bytes 49156
  630.2 47.4 %copy-start.39 = (f32[128,32]{0,1:T(8,128)S(1)}, f32[128,32]{0,1:T(8,128)}, u32[]{:S(2)}) copy-start(f32[128,32]{0,1:T(8,128)} %copy-done.38) | copy-start | bytes 49156
  630.2 47.5 %copy-start.46 = (f32[128,16]{0,1:T(8,128)S(1)}, f32[128,16]{0,1:T(8,128)}, u32[]{:S(2)}) copy-start(f32[128,16]{0,1:T(8,128)} %copy-done.45) | copy-start | bytes 24580
  630.2 47.5 %copy-start.62 = (f32[64]{0:T(128)S(1)}, f32[64]{0:T(128)}, u32[]{:S(2)}) copy-start(f32[64]{0:T(128)} %param.23) | copy-start | bytes 772
  630.2 48.2 %copy-start.51 = (f32[128,16]{0,1:T(8,128)S(1)}, f32[128,16]{0,1:T(8,128)}, u32[]{:S(2)}) copy-start(f32[128,16]{0,1:T(8,128)} %copy-done.50) | copy-start | bytes 24580
  678.6 82.0 %copy-start.26 = (bf16[128,16,64]{0,2,1:T(8,128)(2,1)}, bf16[128,16,64]{0,2,1:T(8,128)(2,1)S(1)}, u32[]{:S(2)}) copy-start(bf16[128,16,64]{0,2,1:T(8,128)(2,1)S(1)} %fusion.114) | copy-start | bytes 786436
  694.8 20.2 %copy-start.5 = (f32[128,8,64]{0,2,1:T(8,128)S(1)}, f32[128,8,64]{0,2,1:T(8,128)}, u32[]{:S(2)}) copy-start(f32[128,8,64]{0,2,1:T(8,128)} %custom-call.4) | copy-start | bytes 786436
  694.8 20.2 %copy-start.14 = (bf16[128,8,64]{0,2,1:T(8,128)(2,1)S(1)}, bf16[128,8,64]{0,2,1:T(8,128)(2,1)}, u32[]{:S(2)}) copy-start(bf16[128,8,64]{0,2,1:T(8,128)(2,1)} %maximum_convert_fusion) | copy-start | bytes 393220
  694.8 20.2 %copy-start.40 = (f32[128,8,64]{0,2,1:T(8,128)S(1)}, f32[128,8,64]{0,2,1:T(8,128)}, u32[]{:S(2)}) copy-start(f32[128,8,64]{0,2,1:T(8,128)} %custom-call.3) | copy-start | bytes 786436
  694.8 20.2 %copy-start.47 = (bf16[128,512]{0,1:T(8,128)(2,1)S(1)}, bf16[128,512]{0,1:T(8,128)(2,1)}, u32[]{:S(2)}) copy-start(bf16[128,512]{0,1:T(8,128)(2,1)} %copy.126) | copy-start | bytes 393220
  715.0 44.8 %copy-start.7 = (f32[128,512]{0,1:T(8,128)S(1)}, f32[128,512]{0,1:T(8,128)}, u32[]{:S(2)}) copy-start(f32[128,512]{0,1:T(8,128)} %copy-done.6) | copy-start | bytes 786436
  715.0 44.8 %copy-start.53 = (f32[128,8]{0,1:T(8,128)S(1)}, f32[128,8]{0,1:T(8,128)}, u32[]{:S(2)}) copy-start(f32[128,8]{0,1:T(8,128)} %copy-done.52) | copy-start | bytes 12292
  715.0 44.8 %copy-start.64 = (f32[64]{0:T(128)S(1)}, f32[64]{0:T(128)}, u32[]{:S(2)}) copy-start(f32[64]{0:T(128)} %param.24) | copy-start | bytes 772
  715.0 45.5 %copy-start.55 = (f32[128,8]{0,1:T(8,128)S(1)}, f32[128,8]{0,1:T(8,128)}, u32[]{:S(2)}) copy-start(f32[128,8]{0,1:T(8,128)} %copy-done.54) | copy-start | bytes 12292
  715.0 45.6 %copy-start.12 = (bf16[1,128,1024]{2,1,0:T(8,128)(2,1)S(1)}, bf16[1,128,1024]{2,1,0:T(8,128)(2,1)}, u32[]{:S(2)}) copy-start(bf16[1,128,1024]{2,1,0:T(8,128)(2,1)} %param.20) | copy-start | bytes 786436
  715.0 45.6 %copy-start.43 = (f32[1024]{0:T(1024)S(1)}, f32[1024]{0:T(1024)}, u32[]{:S(2)}) copy-start(f32[1024]{0:T(1024)} %param.22) | copy-start | bytes 12292
  715.1 45.6 %copy-start.59 = (f32[128]{0:T(128)S(1)}, f32[128]{0:T(128)}, u32[]{:S(2)}) copy-start(f32[128]{0:T(128)} %copy-done.58) | copy-start | bytes 1540
  777.4 343.2 %reduce-scatter.10.cloned.1.call-start = ((), (), s32[]{:S(2)}) async-start(), calls=%async_computation.16 | async-start | bytes 2162688 | tf_op jit(solution)/shard_map/reduce_scatter | solution.py:346
  787.9 414.5 %reduce-scatter.8.cloned.1.call-start = ((), (), s32[]{:S(2)}) async-start(), calls=%async_computation.15 | async-start | bytes 4325376 | tf_op jit(solution)/shard_map/reduce_scatter | solution.py:340
  818.1 593.3 %reduce-scatter.20.cloned.1.call-start = ((), (), s32[]{:S(2)}) async-start(), calls=%async_computation.21 | async-start | bytes 19464192 | tf_op jit(solution)/shard_map/reduce_scatter | solution.py:376
  866.0 756.1 %reduce-scatter.18.cloned.1.call-start = ((), (), s32[]{:S(2)}) async-start(), calls=%async_computation.20 | async-start | bytes 19464192 | tf_op jit(solution)/shard_map/reduce_scatter | solution.py:370
  990.8 841.9 %reduce-scatter.16.cloned.1.call-start = ((), (), s32[]{:S(2)}) async-start(), calls=%async_computation.19 | async-start | bytes 19464192 | tf_op jit(solution)/shard_map/reduce_scatter | solution.py:364
  1079.9 39.7 %copy-start.69 = (f32[128]{0:T(128)S(1)}, f32[128]{0:T(128)}, u32[]{:S(2)}) copy-start(f32[128]{0:T(128)} %copy-done.68) | copy-start | bytes 1540
  1079.9 39.7 %copy-start.16 = (f32[128,1024]{1,0:T(8,128)S(1)}, f32[128,1024]{1,0:T(8,128)}, u32[]{:S(2)}) copy-start(f32[128,1024]{1,0:T(8,128)} %copy-done.15) | copy-start | bytes 1572868
  (43 other events, 201.3 us)
Sparse Core Ops, SparseCore 0:
  11.9 59.4 all-gather.8
  77.2 41.1 all-gather.12
  121.2 40.3 all-gather.10
  163.0 31.8 all-gather.14
  196.3 224.3 all-gather.16
  422.1 117.9 all-gather.18
  542.9 53.1 all-gather.20
  598.3 48.7 all-gather.22
  649.9 139.8 reduce-scatter.13
  792.4 133.4 reduce-scatter.11
  928.9 132.8 reduce-scatter.9
  1064.5 137.8 reduce-scatter.7
  1209.4 201.9 reduce-scatter.19
  1418.2 203.7 reduce-scatter.17
  1628.9 203.7 reduce-scatter.15
where the time goes:
time: 1850 us; the launch traced here: 1840 us
  waiting for transfers between devices  1190 us (64%)
  local copies, waits for them, and re-layouts  390 us (21%)
  matrix products  141 us (8%)
  blocking collectives  56.8 us (3%)
  other arithmetic  42.4 us (2%)
    all_gather x1, waiting for transfers between devices, local(): lax.all_gather(glu_local, 'fsdp', axis=0, tiled=True)  223 us
    reduce_scatter x1, waiting for transfers between devices, local(): lax.psum_scatter(arrange_blocks(up_term, cycle_count, pair_count), ('ctx'...  211 us
    reduce_scatter x1, waiting for transfers between devices, local(): lax.psum_scatter(arrange_blocks(gate_term, cycle_count, pair_count), ('ct...  211 us
    reduce_scatter x1, waiting for transfers between devices, local(): lax.psum_scatter(arrange_blocks(down_term, cycle_count, pair_count), ('ct...  209 us
    all_gather x1, waiting for transfers between devices, local(): lax.all_gather(down_local, 'fsdp', axis=0, tiled=True)  107 us
    reshape x7, local copies, waits for them, and re-layouts, arrange_blocks(): jnp.transpose(shaped, (2, 0, 1, 3))  88.8 us
    reduce_scatter x1, waiting for transfers between devices, local(): lax.psum_scatter(arrange_blocks(query_term, cycle_count, pair_count), ('c...  81.8 us
    transpose x7, local copies, waits for them, and re-layouts, arrange_blocks(): jnp.transpose(shaped, (2, 0, 1, 3))  67 us
  transfers between devices with their start and end apart: 15, of which 11 were waited for; matrix products, arithmetic and copies ran while one was open for 30% of the time, Pallas kernels for 0%

commit v1 on v0

v1 whole, which is shorter than its diff:
```python
import functools

import jax
import jax.numpy as jnp
from jax import lax
from jax.experimental import pallas as pl
from jax.experimental.pallas import tpu as pltpu
from jax.sharding import PartitionSpec as P

QUERY_HEADS = 16
KEY_VALUE_HEADS = 8
HEAD_SIZE = 64
FF = 4608
WIDTH = 1024
GROUP = 4
ROWS = 128

epsilon = 1e-05
rope_base = 1000000.0
MESH = pl.DeviceIdType.MESH
ANY = pl.ANY
bf16 = jnp.bfloat16
f32 = jnp.float32


def who():
    c = lax.axis_index("ctx")
    f = lax.axis_index("fsdp")
    return c, f, lax.rem(c, GROUP)


def flip(l, k):
    if k == 0:
        return l
    if k == 1:
        return l + 1 - 2 * lax.rem(l, 2)
    return lax.rem(l + 2, GROUP)


KINDS = ((2, 0), (0, 1), (2, 1))


def slot(l, f):
    return f * GROUP + l


def enter(peers):
    bar = pltpu.get_barrier_semaphore()
    for p in peers:
        pl.semaphore_signal(bar, inc=1, device_id=p, device_id_type=MESH)
    pl.semaphore_wait(bar, len(peers))


def rcopy(src, dst, s, r, dev):
    return pltpu.make_async_remote_copy(
        src_ref=src, dst_ref=dst, send_sem=s, recv_sem=r, device_id=dev, device_id_type=MESH
    )


def gather8_kernel(x_ref, o_ref, ss, rs, ls):
    c, f, l = who()
    base = c - l
    sib = (base + flip(l, 1), f)
    peers = [(base + flip(l, a), lax.rem(f + b, 2)) for a, b in KINDS]
    me = slot(l, f)
    own = pltpu.make_async_copy(x_ref, o_ref.at[me], ls)
    own.start()
    enter([sib] + peers)
    first = []
    for k, p in enumerate(peers):
        cp = rcopy(x_ref, o_ref.at[me], ss.at[k], rs.at[k], p)
        cp.start()
        first.append(cp)
    cp0 = rcopy(x_ref, o_ref.at[me], ss.at[3], rs.at[3], sib)
    cp0.start()
    fw = []
    for k, (a, b) in enumerate(KINDS):
        sl = slot(flip(l, a), lax.rem(f + b, 2))
        first[k].wait_recv()
        cp = rcopy(o_ref.at[sl], o_ref.at[sl], ss.at[4 + k], rs.at[4 + k], sib)
        cp.start()
        fw.append(cp)
    for cp in fw + [cp0]:
        cp.wait_recv()
    for cp in first + [cp0] + fw:
        cp.wait_send()
    own.wait()


def comm_params(cid):
    return pltpu.CompilerParams(collective_id=cid, has_side_effects=True)


def any_specs(n):
    return [pl.BlockSpec(memory_space=ANY)] * n


def gather8(x, cid):
    return pl.pallas_call(
        gather8_kernel,
        out_shape=jax.ShapeDtypeStruct((8,) + x.shape, x.dtype),
        in_specs=any_specs(1),
        out_specs=any_specs(1)[0],
        scratch_shapes=[
            pltpu.SemaphoreType.DMA((7,)),
            pltpu.SemaphoreType.DMA((7,)),
            pltpu.SemaphoreType.DMA,
        ],
        compiler_params=comm_params(cid),
        name="gather8_%d" % cid,
    )(x)


def line_kernel(n, same, x_ref, o_ref, ss, rs, ls):
    c, f, l = who()
    t = lax.div(c, GROUP)
    peers = [(lax.rem(t + s, n) * GROUP + l, f) for s in range(1, n)]

    def src(tt):
        return x_ref if same else x_ref.at[tt]

    own = pltpu.make_async_copy(src(t), o_ref.at[t], ls)
    own.start()
    enter(peers)
    cps = []
    for s in range(1, n):
        cp = rcopy(src(lax.rem(t + s, n)), o_ref.at[t], ss.at[s - 1], rs.at[s - 1], peers[s - 1])
        cp.start()
        cps.append(cp)
    for cp in cps:
        cp.wait_recv()
    for cp in cps:
        cp.wait_send()
    own.wait()


def line(x, n, same, cid):
    shp = x.shape if same else x.shape[1:]
    return pl.pallas_call(
        functools.partial(line_kernel, n, same),
        out_shape=jax.ShapeDtypeStruct((n,) + shp, x.dtype),
        in_specs=any_specs(1),
        out_specs=any_specs(1)[0],
        scratch_shapes=[
            pltpu.SemaphoreType.DMA((n - 1,)),
            pltpu.SemaphoreType.DMA((n - 1,)),
            pltpu.SemaphoreType.DMA,
        ],
        compiler_params=comm_params(cid),
        name="line_%d" % cid,
    )(x)


def scatter8_kernel(x_ref, o_ref, a, b, s_buf, d, ls, s1, r1, s2, r2):
    c, f, l = who()
    base = c - l
    sl = flip(l, 1)
    sib = (base + sl, f)
    peers = [(base + flip(l, i), lax.rem(f + j, 2)) for i, j in KINDS]
    kinds = list(KINDS) + [(0, 0)]
    loads = []
    for k, (i, j) in enumerate(kinds):
        cp = pltpu.make_async_copy(
            x_ref.at[slot(flip(l, i), lax.rem(f + j, 2))], a.at[k], ls.at[k]
        )
        cp.start()
        loads.append(cp)
    enter([sib] + peers)
    ones = []
    for k, (i, j) in enumerate(kinds):
        cp = rcopy(
            x_ref.at[slot(flip(sl, i), lax.rem(f + j, 2))], b.at[k], s1.at[k], r1.at[k], sib
        )
        cp.start()
        ones.append(cp)
    twos = []
    for k in range(3):
        loads[k].wait()
        ones[k].wait_recv()
        s_buf[k] = (a[k].astype(f32) + b[k].astype(f32)).astype(s_buf.dtype)
        cp = rcopy(s_buf.at[k], d.at[k], s2.at[k], r2.at[k], peers[k])
        cp.start()
        twos.append(cp)
    loads[3].wait()
    ones[3].wait_recv()
    total = a[3].astype(f32) + b[3].astype(f32)
    for k in range(3):
        twos[k].wait_recv()
        total = total + d[k].astype(f32)
    o_ref[...] = total
    for cp in ones + twos:
        cp.wait_send()


def scatter8(x, cid):
    shp = x.shape[1:]
    return pl.pallas_call(
        scatter8_kernel,
        out_shape=jax.ShapeDtypeStruct(shp, f32),
        in_specs=any_specs(1),
        out_specs=pl.BlockSpec(memory_space=pltpu.VMEM),
        scratch_shapes=[
            pltpu.VMEM((4,) + shp, x.dtype),
            pltpu.VMEM((4,) + shp, x.dtype),
            pltpu.VMEM((3,) + shp, x.dtype),
            pltpu.VMEM((3,) + shp, x.dtype),
            pltpu.SemaphoreType.DMA((4,)),
            pltpu.SemaphoreType.DMA((4,)),
            pltpu.SemaphoreType.DMA((4,)),
            pltpu.SemaphoreType.DMA((3,)),
            pltpu.SemaphoreType.DMA((3,)),
        ],
        compiler_params=comm_params(cid),
        name="scatter8_%d" % cid,
    )(x)


def swap8_kernel(x_ref, o_ref, ss, rs, ls):
    c, f, l = who()
    base = c - l
    me = slot(l, f)
    own = pltpu.make_async_copy(x_ref.at[me], o_ref.at[me], ls)
    own.start()
    others = [(i, j) for j in range(2) for i in range(4) if i + j]
    peers = [(base + lax.rem(l + i, GROUP), lax.rem(f + j, 2)) for i, j in others]
    enter(peers)
    cps = []
    for k, (i, j) in enumerate(others):
        to = slot(lax.rem(l + i, GROUP), lax.rem(f + j, 2))
        cp = rcopy(x_ref.at[to], o_ref.at[me], ss.at[k], rs.at[k], peers[k])
        cp.start()
        cps.append(cp)
    for cp in cps:
        cp.wait_recv()
    for cp in cps:
        cp.wait_send()
    own.wait()


def swap8(x, cid):
    return pl.pallas_call(
        swap8_kernel,
        out_shape=jax.ShapeDtypeStruct(x.shape, x.dtype),
        in_specs=any_specs(1),
        out_specs=any_specs(1)[0],
        scratch_shapes=[
            pltpu.SemaphoreType.DMA((7,)),
            pltpu.SemaphoreType.DMA((7,)),
            pltpu.SemaphoreType.DMA,
        ],
        compiler_params=comm_params(cid),
        name="swap8_%d" % cid,
    )(x)


def back_product(left, right):
    return lax.dot_general(
        left, right, (((1,), (1,)), ((), ())), preferred_element_type=f32
    )


def lead_sum(left, right):
    return lax.dot_general(
        left, right, (((0,), (0,)), ((), ())), preferred_element_type=f32
    )


def dot(left, right):
    return jnp.dot(left, right, preferred_element_type=f32)


def allowed_block(begin_ref, tok0, key0, rows, keys):
    token = tok0 + lax.broadcasted_iota(jnp.int32, (rows, keys), 0)
    key = key0 + lax.broadcasted_iota(jnp.int32, (rows, keys), 1)
    return (key >= begin_ref) & (key <= token)


def attend_kernel(t_ref, q_ref, kv_ref, begin_ref, sum_ref, tot_ref):
    t = t_ref[0]
    half = q_ref.shape[0] // 2
    qb = 256
    for s in range(2):
        for h in range(2):
            for b in range(half // qb):
                r0 = s * half + b * qb
                q = q_ref[r0 : r0 + qb, h * 64 : h * 64 + 64]
                begin = begin_ref[r0 : r0 + qb, :]

                def step(tt, carry):
                    acc, tot = carry
                    kb = kv_ref[tt, s * half : (s + 1) * half, :]
                    sc = back_product(q, kb[:, :64])
                    ok = allowed_block(begin, t * half + b * qb, tt * half, qb, half)
                    e = jnp.where(ok, jnp.exp(sc), 0.0)
                    acc = acc + dot(e.astype(bf16), kb[:, 64:])
                    tot = tot + jnp.sum(e, axis=1, keepdims=True)
                    return acc, tot

                acc, tot = lax.fori_loop(
                    0,
                    t + 1,
                    step,
                    (jnp.zeros((qb, 64), f32), jnp.zeros((qb, 1), f32)),
                )
                sum_ref[r0 : r0 + qb, h * 64 : h * 64 + 64] = acc
                tot_ref[r0 : r0 + qb, h * 64 : h * 64 + 64] = jnp.broadcast_to(tot, (qb, 64))


VM = pltpu.VMEM


def vspecs(n):
    return [pl.BlockSpec(memory_space=VM)] * n


def attend(t, q, kv, begin):
    n = q.shape[0]
    return pl.pallas_call(
        attend_kernel,
        out_shape=(jax.ShapeDtypeStruct((n, 128), f32), jax.ShapeDtypeStruct((n, 128), f32)),
        in_specs=[pl.BlockSpec(memory_space=pltpu.SMEM)] + vspecs(3),
        out_specs=tuple(vspecs(2)),
        cost_estimate=pl.CostEstimate(flops=2**31, bytes_accessed=2**22, transcendentals=2**22),
        compiler_params=pltpu.CompilerParams(vmem_limit_bytes=40 * 2**20),
        name="attend",
    )(t, q, kv, begin)


def attend_back_kernel(t_ref, q_ref, kv_ref, begin_ref, g_ref, delta_ref, dq_ref, dkv_ref):
    t = t_ref[0]
    half = q_ref.shape[0] // 2
    qb = 256
    T = kv_ref.shape[0]

    def clear(tt, _):
        dkv_ref[tt] = jnp.zeros(dkv_ref.shape[1:], dkv_ref.dtype)
        return 0

    lax.fori_loop(t + 1, T, clear, 0)
    dq_ref[...] = jnp.zeros_like(dq_ref)
    for s in range(2):

        def step(tt, _):
            kb = kv_ref[tt, s * half : (s + 1) * half, :]
            dk = jnp.zeros((half, 64), f32)
            dv = jnp.zeros((half, 64), f32)
            for h in range(2):
                for b in range(half // qb):
                    r0 = s * half + b * qb
                    rows = slice(r0, r0 + qb)
                    lanes = slice(h * 64, h * 64 + 64)
                    q = q_ref[rows, lanes]
                    g = g_ref[rows, lanes]
                    sc = back_product(q, kb[:, :64])
                    ok = allowed_block(
                        begin_ref[rows, :], t * half + b * qb, tt * half, qb, half
                    )
                    e = jnp.where(ok, jnp.exp(sc), 0.0)
                    dp = back_product(g, kb[:, 64:])
                    ds = (e * (dp - delta_ref[rows, h * 64 : h * 64 + 1])).astype(bf16)
                    dq_ref[rows, lanes] += dot(ds, kb[:, :64])
                    dk = dk + lead_sum(ds, q)
                    dv = dv + lead_sum(e.astype(bf16), g)
            dkv_ref[tt, s * half : (s + 1) * half, :] = jnp.concatenate([dk, dv], axis=1).astype(
                dkv_ref.dtype
            )
            return 0

        lax.fori_loop(0, t + 1, step, 0)


def attend_back(t, q, kv, begin, g, delta):
    n = q.shape[0]
    return pl.pallas_call(
        attend_back_kernel,
        out_shape=(jax.ShapeDtypeStruct((n, 128), f32), jax.ShapeDtypeStruct(kv.shape, bf16)),
        in_specs=[pl.BlockSpec(memory_space=pltpu.SMEM)] + vspecs(5),
        out_specs=tuple(vspecs(2)),
        cost_estimate=pl.CostEstimate(flops=2**33, bytes_accessed=2**23, transcendentals=2**22),
        compiler_params=pltpu.CompilerParams(vmem_limit_bytes=48 * 2**20),
        name="attend_back",
    )(t, q, kv, begin, g, delta)


def root_mean_norm(rows, gain):
    return (
        rows * lax.rsqrt(jnp.mean(rows * rows, axis=-1, keepdims=True) + epsilon) * gain
    )


def rotary(rows, cosine, sine):
    halfway = rows.shape[-1] // 2
    leading = rows[..., :halfway]
    trailing = rows[..., halfway:]
    return jnp.concatenate(
        [leading * cosine - trailing * sine, leading * sine + trailing * cosine], axis=-1
    )


SWAP = [(0, 1), (1, 0)]


def halves(f, own, other, axis):
    return jnp.where(
        f == 0,
        jnp.concatenate([own, other], axis=axis),
        jnp.concatenate([other, own], axis=axis),
    )


def local(
    hidden_in,
    doc_lengths,
    attn_gain,
    query_gain,
    key_norm_gain,
    ffn_gain,
    query_proj,
    key_weight,
    value_weight,
    attn_proj,
    gate_proj,
    up_proj,
    down_proj,
    out_cotangent,
):
    n_ctx = lax.axis_size("ctx")
    T = n_ctx // GROUP
    c = lax.axis_index("ctx")
    f = lax.axis_index("fsdp")
    t = c // GROUP
    l = c % GROUP
    head = slot(l, f)
    other_head = slot(l, 1 - f)
    tokens = 8 * ROWS
    half_tokens = tokens // 2
    segment = FF // n_ctx // 2
    columns = T * segment
    half_width = WIDTH // 2

    def head_columns(j):
        return jnp.concatenate(
            [
                lax.dynamic_slice(query_proj, (0, j * 128), (half_width, 128)),
                lax.dynamic_slice(key_weight, (0, j * 64), (half_width, 64)),
                lax.dynamic_slice(value_weight, (0, j * 64), (half_width, 64)),
            ],
            axis=1,
        ).astype(bf16)

    def ff_columns(ff):
        parts = []
        for w in (gate_proj, up_proj):
            for tt in range(T):
                parts.append(
                    lax.dynamic_slice(
                        w,
                        (0, (GROUP * tt + l) * 2 * segment + ff * segment),
                        (half_width, segment),
                    )
                )
        return jnp.concatenate(parts, axis=1).astype(bf16)

    def ff_rows(ff):
        parts = [
            lax.dynamic_slice(
                down_proj, ((GROUP * tt + l) * 2 * segment + ff * segment, 0), (segment, WIDTH)
            )
            for tt in range(T // 2)
        ]
        return jnp.concatenate(parts, axis=0).astype(bf16)

    w_heads = halves(
        f, head_columns(head), lax.ppermute(head_columns(other_head), "fsdp", SWAP), 0
    )
    out_own = attn_proj.astype(bf16)
    w_out = halves(f, out_own, lax.ppermute(out_own, "fsdp", SWAP), 0)
    w_glu = halves(f, ff_columns(f), lax.ppermute(ff_columns(1 - f), "fsdp", SWAP), 0)
    w_down = halves(f, ff_rows(f), lax.ppermute(ff_rows(1 - f), "fsdp", SWAP), 0)

    lengths_other = lax.ppermute(doc_lengths, "fsdp", SWAP)
    lengths = halves(f, doc_lengths, lengths_other, 0)
    starts = jnp.cumsum(lengths, axis=1) - lengths
    token_index = t * half_tokens + jnp.arange(half_tokens, dtype=jnp.int32)
    after = token_index[None, :, None] >= starts[:, None, :]
    begins = jnp.max(jnp.where(after, starts[:, None, :], 0), axis=2).reshape(tokens, 1)
    place = jnp.concatenate([token_index, token_index])[:, None] - begins
    freqs = rope_base ** (-2.0 * jnp.arange(32, dtype=f32) / 64)
    angles = place.astype(f32) * freqs[None, :]
    cosine = jnp.cos(angles)[:, None, :]
    sine = jnp.sin(angles)[:, None, :]

    both = gather8(jnp.stack([hidden_in[0], out_cotangent[0]]), 1)
    x_all = both[:, 0].reshape(tokens, WIDTH).astype(f32)
    c_all = both[:, 1].reshape(tokens, WIDTH)

    normed = root_mean_norm(x_all, attn_gain).astype(bf16)
    stacked = dot(normed, w_heads)

    def rotate(q_in, k_in, q_gain, k_gain):
        q_out = (
            rotary(root_mean_norm(q_in.reshape(tokens, 2, HEAD_SIZE), q_gain), cosine, sine)
            * HEAD_SIZE ** (-0.5)
        )
        k_out = rotary(root_mean_norm(k_in.reshape(tokens, 1, HEAD_SIZE), k_gain), cosine, sine)
        return q_out.reshape(tokens, 128), k_out.reshape(tokens, 64)

    (q_rot, k_rot), heads_back = jax.vjp(
        rotate, stacked[:, :128], stacked[:, 128:192], query_gain, key_norm_gain
    )
    q_rows = q_rot.astype(bf16)
    kv_rows = jnp.concatenate([k_rot, stacked[:, 192:]], axis=1).astype(bf16)
    kv_all = line(kv_rows, T, True, 2)
    t_arr = jnp.full((1,), t, jnp.int32)
    summed, totals = attend(t_arr, q_rows, kv_all, begins)
    attended = gather8((summed / totals).astype(bf16), 3)
    attended = jnp.transpose(attended, (1, 0, 2)).reshape(tokens, WIDTH)
    middle = x_all + dot(attended, w_out)
    normed_ffn = root_mean_norm(middle, ffn_gain).astype(bf16)
    glu = dot(normed_ffn, w_glu)
    gate = glu[:, :columns]
    up = glu[:, columns:]
    sig = 1.0 / (1.0 + jnp.exp(-gate))
    silu = gate * sig
    hidden = (silu * up).astype(bf16)
    grad_hidden = back_product(c_all, w_down)
    grad_gate = (grad_hidden * up * (sig * (1.0 + gate * (1.0 - sig)))).astype(bf16)
    grad_up = (grad_hidden * silu).astype(bf16)
    grad_glu = jnp.concatenate([grad_gate, grad_up], axis=1)
    part_in = back_product(grad_glu, w_glu)
    part_out = dot(hidden, w_down)
    parts = jnp.stack(
        [part_in.reshape(8, ROWS, WIDTH), part_out.reshape(8, ROWS, WIDTH)], axis=1
    ).astype(bf16)
    own_sums = scatter8(parts, 4)

    own = lax.dynamic_slice(middle, (head * ROWS, 0), (ROWS, WIDTH))
    output = own + own_sums[1]
    _, ffn_back = jax.vjp(root_mean_norm, own, ffn_gain)
    grad_mid_norm, ffn_gain_part = ffn_back(own_sums[0])
    grad_middle = out_cotangent[0].astype(f32) + grad_mid_norm
    branch = gather8(grad_middle.astype(bf16), 5).reshape(tokens, WIDTH)

    w_out_head = lax.dynamic_slice(out_own, (l * 128, 0), (128, WIDTH))
    grad_mixed = back_product(branch, w_out_head)
    grad_summed = (grad_mixed / totals).astype(bf16)
    weighted = (grad_mixed * summed / (totals * totals)).reshape(tokens, 2, 64)
    delta = jnp.broadcast_to(
        jnp.sum(weighted, axis=2, keepdims=True), (tokens, 2, 64)
    ).reshape(tokens, 128)
    grad_q, dkv = attend_back(t_arr, q_rows, kv_all, begins, grad_summed, delta)
    dkv = jnp.sum(line(dkv, T, False, 6).astype(f32), axis=0)
    gq_pre, gk_pre, q_gain_part, k_gain_part = heads_back((grad_q, dkv[:, :64]))
    grad_stacked = jnp.concatenate([gq_pre, gk_pre, dkv[:, 64:]], axis=1).astype(bf16)
    part_normed = back_product(grad_stacked, w_heads).reshape(8, ROWS, WIDTH).astype(bf16)
    grad_normed = scatter8(part_normed, 7)
    _, attn_back = jax.vjp(root_mean_norm, hidden_in[0].astype(f32), attn_gain)
    grad_resid, attn_gain_part = attn_back(grad_normed)
    input_grad = grad_middle + grad_resid

    glu_part = lead_sum(grad_glu, normed_ffn)
    glu_part = jnp.transpose(
        glu_part.reshape(2, T, segment, WIDTH).astype(bf16), (1, 0, 2, 3)
    )
    down_part = lead_sum(hidden, c_all)
    down_part = jnp.transpose(
        down_part.astype(bf16).reshape(columns, T, WIDTH // T), (1, 0, 2)
    )
    glu_sum = jnp.sum(line(glu_part, T, False, 8).astype(f32), axis=0)
    down_sum = jnp.sum(line(down_part, T, False, 9).astype(f32), axis=0)
    keep = lax.dynamic_slice(glu_sum, (0, 0, f * half_width), (2, segment, half_width))
    give = lax.dynamic_slice(glu_sum, (0, 0, (1 - f) * half_width), (2, segment, half_width))
    glu_grad = halves(f, keep, lax.ppermute(give, "fsdp", SWAP), 1)
    gate_grad = jnp.transpose(glu_grad[0])
    up_grad = jnp.transpose(glu_grad[1])

    each = WIDTH // n_ctx
    pieces = down_sum.reshape(2, columns // 2, GROUP, each)
    pieces = jnp.transpose(pieces, (0, 2, 1, 3)).reshape(8, columns // 2, each)
    got = swap8(pieces, 10).reshape(2, GROUP, T // 2, segment, each)
    down_grad = jnp.transpose(got, (2, 1, 0, 3, 4)).reshape(FF // 2, each)

    attended_half = lax.dynamic_slice(attended, (0, f * half_width), (tokens, half_width))
    branch_columns = lax.dynamic_slice(
        branch.reshape(tokens, T, GROUP, each), (0, 0, l, 0), (tokens, T, 1, each)
    ).reshape(tokens, T * each)
    attn_part = lead_sum(attended_half, branch_columns).astype(bf16)
    attn_part = jnp.transpose(attn_part.reshape(half_width, T, each), (1, 0, 2))
    attn_grad = jnp.sum(line(attn_part, T, False, 11).astype(f32), axis=0)

    heads_part = lead_sum(normed, grad_stacked).astype(bf16).reshape(T, WIDTH // T, 256)
    heads_sum = jnp.sum(line(heads_part, T, False, 12).astype(f32), axis=0)
    many = T // 2
    kw = 64 // many
    q_pieces = heads_sum[:, :128].reshape(WIDTH // T, many, 128 // many)
    k_pieces = heads_sum[:, 128:192].reshape(WIDTH // T, many, kw)
    v_pieces = heads_sum[:, 192:].reshape(WIDTH // T, many, kw)
    all_pieces = jnp.transpose(
        jnp.concatenate([q_pieces, k_pieces, v_pieces], axis=2), (1, 0, 2)
    )
    rows_of = []
    for i in range(many):
        perm = []
        for src_t in range(T):
            for src_l in range(GROUP):
                for src_f in range(2):
                    to_ctx = slot(src_l, src_f) * many + (i + src_t) % many
                    perm.append(((src_t * GROUP + src_l) * 2 + src_f, to_ctx * 2 + src_t // many))
        piece = lax.dynamic_index_in_dim(all_pieces, (i + t) % many, 0, keepdims=False)
        rows_of.append(lax.ppermute(piece, ("ctx", "fsdp"), perm))
    got_rows = jnp.stack(rows_of)
    order = (c - jnp.arange(many)) % many
    heads_grad = jnp.take(got_rows, order, axis=0).reshape(half_width, 256 // many)
    query_grad = heads_grad[:, : 128 // many]
    key_grad = heads_grad[:, 128 // many : 128 // many + kw]
    value_grad = heads_grad[:, 128 // many + kw :]

    gains = jnp.concatenate([attn_gain_part, ffn_gain_part, q_gain_part, k_gain_part])
    gains = jnp.sum(gather8(gains.reshape(17, 128), 13), axis=0)
    gains = jnp.sum(line(gains, T, True, 14), axis=0).reshape(-1)
    return (
        output[None],
        input_grad[None],
        gains[:WIDTH],
        gains[2 * WIDTH : 2 * WIDTH + 64],
        gains[2 * WIDTH + 64 :],
        gains[WIDTH : 2 * WIDTH],
        query_grad,
        key_grad,
        value_grad,
        attn_grad,
        gate_grad,
        up_grad,
        down_grad,
    )


def solution(mesh):
    in_specs = (
        P("fsdp", "ctx", None),
        P("fsdp", None),
        P(),
        P(),
        P(),
        P(),
        P("fsdp", None),
        P("fsdp", None),
        P("fsdp", None),
        P("fsdp", None),
        P("fsdp", None),
        P("fsdp", None),
        P("fsdp", None),
        P("fsdp", "ctx", None),
    )
    out_specs = (
        P("fsdp", "ctx", None),
        P("fsdp", "ctx", None),
        P(),
        P(),
        P(),
        P(),
        P("fsdp", "ctx"),
        P("fsdp", "ctx"),
        P("fsdp", "ctx"),
        P("fsdp", "ctx"),
        P("fsdp", "ctx"),
        P("fsdp", "ctx"),
        P("fsdp", "ctx"),
    )
    return jax.shard_map(local, mesh=mesh, in_specs=in_specs, out_specs=out_specs, check_vma=False)
```

time: 1850 us -> 565 us (0.31)
  the two profiles are of different devices: /device:TPU:0 before, /device:TPU:9 now
where the time goes in v1:
time: 565 us; the launch traced here: 554 us
  Pallas kernels  381 us (67%)
  local copies, waits for them, and re-layouts  64.2 us (11%)
  other arithmetic  51.1 us (9%)
  matrix products  43.5 us (8%)
  starting transfers between devices  11.5 us (2%)
    pallas_call x7, Pallas kernels, line(): pl.pallas_call(functools.partial(line_kernel, n, same), out_shape=jax.Sha...  184 us
    pallas_call x4, Pallas kernels, gather8(): pl.pallas_call(gather8_kernel, out_shape=jax.ShapeDtypeStruct((8,) + x.sh...  118 us
    pallas_call x2, Pallas kernels, scatter8(): pl.pallas_call(scatter8_kernel, out_shape=jax.ShapeDtypeStruct(shp, f32),...  46.7 us
    dot_general x4, matrix products, dot(): return jnp.dot(left, right, preferred_element_type=f32)  17.5 us
    pallas_call x1, Pallas kernels, swap8(): pl.pallas_call(swap8_kernel, out_shape=jax.ShapeDtypeStruct(x.shape, x.dt...  17.1 us
    dot_general x4, matrix products, back_product(): lax.dot_general(left, right, (((1,), (1,)), ((), ())), preferred_element_...  14.7 us
    another operation x7, local copies, waits for them, and re-layouts  13.9 us
  transfers between devices with their start and end apart: 8, of which 0 were waited for; matrix products, arithmetic and copies ran while one was open for 17% of the time, Pallas kernels for 39%

profile of v1, /device:TPU:9, one launch (start us, length us, event | category | flops | bytes accessed | tf_op | source)
XLA Modules:
  0.0 554.0 jit_solution(11605588298409799067)
XLA Ops:
  2.6 2.1 dynamic-slice_convert_fusion.23
  9.3 7.2 %dynamic-slice_convert_fusion.12 = (bf16[512,144]{1,0:T(8,128)(2,1)S(1)}, bf16[512,144]{1,0:T(8,128)(2,1)S(1)}, bf16[512,144]{1,0:T(8,128)(2,1)S(1)}, bf16[512,1...) fusion(f32[512,4608]{1,0:T(8,128)} %param.25, ...), kind=kLoop, calls=%fused_computation.116 | loop fusion | bytes 4718624 | tf_op jit(solution)/shard_map/convert.28
  16.5 3.7 concatenate.123
  20.5 2.6 dynamic-slice_convert_fusion.3
  26.0 74.0 %gather8_1.1 = bf16[8,2,128,1024]{3,2,1,0:T(8,128)(2,1)} custom-call(bf16[2,128,1024]{2,1,0:T(8,128)(2,1)} %pad_maximum_fusion.5.x_ref), custom_call_target="tpu_custom_call" | custom-call | tf_op jit(solution)/shard_map/gather8_1/pallas_call | solution.py:99
  100.0 2.1 fusion.1
  102.1 4.8 fusion.64
  108.9 3.6 fusion.3
  112.4 2.3 concatenate.122
  115.9 2.7 fusion.63
  120.6 3.8 fusion.22
  126.6 26.6 %line_2.1.kv_ref = bf16[4,1024,128]{2,1,0:T(8,128)(2,1)} custom-call(bf16[1024,128]{1,0:T(8,128)(2,1)} %pad_maximum_fusion.8.x_ref), custom_call_target="tpu_custom_call" | custom-call | tf_op jit(solution)/shard_map/line_2/pallas_call | solution.py:139
  154.4 7.8 %attend.1 = (f32[1024,128]{1,0:T(8,128)S(1)}, f32[1024,128]{1,0:T(8,128)S(1)}) custom-call(s32[1]{0:T(128)} %bitcast.1.t_ref, bf16[1024,128]{1,0:T(8,128)(2,1)S(1)} %copy.129.q_ref, bf16[4,1024,128]{2,1,0:T(8,128)(2,1)S(1)} %copy-done, s32[1024,1]{1,0:T(8,128)S(1)} %bitcast.148), custom_call_target="tpu_custom_call" | custom-call | flops 2147483648 | bytes 4194304 | tf_op jit(solution)/shard_map/attend/pallas_call | solution.py:318
  163.0 17.3 %gather8_3.1 = bf16[8,1024,128]{2,1,0:T(8,128)(2,1)} custom-call(bf16[1024,128]{1,0:T(8,128)(2,1)} %divide_convert_fusion.1.x_ref), custom_call_target="tpu_custom_call" | custom-call | tf_op jit(solution)/shard_map/gather8_3/pallas_call | solution.py:99
  180.4 4.2 copy.131
  184.6 6.4 %multiply_reduce_fusion = (f32[1024]{0:T(1024)S(1)}, f32[1024,1024]{1,0:T(8,128)S(1)}) fusion(bf16[1024,1024]{0,1:T(8,128)(2,1)} %bitcast.160, bf16[512,1024]{1,0:T(8,128)(2,1)} %collective-permute-done.2, bf16[512,1024]{1,0:T(8,128)(2,1)} %convert_element_type.113, pred[]{:T(512)S(6)} %eq.7, bf16[8,1,128,1024]{3,2,1,0:T(8,128)(2,1)} %get-tuple-element.94), kind=kOutput, calls=%fused_computation.11 | convolution fusion | flops 2161114112 | bytes 10489857 | tf_op jit(solution)/shard_map/dot_general | solution.py:269
  192.0 5.3 fusion.41
  197.3 3.5 multiply_convert_fusion.3
  200.9 4.2 convolution_convert_fusion
  205.0 4.8 convolution_convert_fusion.1
  209.9 3.1 convolution_convert_fusion.3
  213.0 2.4 pad_maximum_fusion.x_ref
  215.4 29.9 %scatter8_4.1 = f32[2,128,1024]{2,1,0:T(8,128)} custom-call(bf16[8,2,128,1024]{3,2,1,0:T(8,128)(2,1)} %pad_maximum_fusion.x_ref), custom_call_target="tpu_custom_call" | custom-call | tf_op jit(solution)/shard_map/scatter8_4/pallas_call | solution.py:197
  245.3 1.9 fusion.39
  248.4 2.1 fusion.62.x_ref
  250.5 17.1 %gather8_5.1 = bf16[8,128,1024]{2,1,0:T(8,128)(2,1)} custom-call(bf16[128,1024]{1,0:T(8,128)(2,1)} %fusion.62.x_ref), custom_call_target="tpu_custom_call" | custom-call | tf_op jit(solution)/shard_map/gather8_5/pallas_call | solution.py:99
  267.6 4.2 copy.150
  271.8 3.1 multiply_divide_fusion
  278.2 8.5 %attend_back.1 = (f32[1024,128]{1,0:T(8,128)S(1)}, bf16[4,1024,128]{2,1,0:T(8,128)(2,1)S(1)}) custom-call(s32[1]{0:T(128)} %bitcast.1.t_ref, bf16[1024,128]{1,0:T(8,128)(2,1)S(1)} %copy.129.q_ref, bf16[4,1024,128]{2,1,0:T(8,128)(2,1)S(1)} %copy-done, s32[1024,1]{1,0:T(8,128)S(1)} %bitcast.149, bf16[1024,128]{1,0:T(8,128)(2,1)S(1)} %get-tuple-element.102.g_ref, ...), custom_call_target="tpu_custom_call" | custom-call | flops 8589934592 | bytes 8388608 | tf_op jit(solution)/shard_map/attend_back/pallas_call | solution.py:374
  287.6 41.1 %line_6.1 = bf16[4,1024,128]{2,1,0:T(8,128)(2,1)} custom-call(bf16[4,1024,128]{2,1,0:T(8,128)(2,1)} %copy-done.1), custom_call_target="tpu_custom_call" | custom-call | tf_op jit(solution)/shard_map/line_6/pallas_call | solution.py:139
  337.3 2.4 fusion.25
  343.0 14.7 %line_12.1 = bf16[4,256,256]{2,1,0:T(8,128)(2,1)} custom-call(bf16[4,256,256]{2,1,0:T(8,128)(2,1)} %bitcast.173), custom_call_target="tpu_custom_call" | custom-call | tf_op jit(solution)/shard_map/line_12/pallas_call | solution.py:139
  359.0 3.8 convolution_convert_fusion.4
  364.5 52.6 %line_8.1 = bf16[4,2,144,1024]{3,2,1,0:T(8,128)(2,1)} custom-call(bf16[4,2,144,1024]{3,2,1,0:T(8,128)(2,1)} %bitcast.150), custom_call_target="tpu_custom_call" | custom-call | tf_op jit(solution)/shard_map/line_8/pallas_call | solution.py:139
  417.2 2.4 convert_reduce_fusion
  421.8 2.3 reshape_reshape.3
  428.1 13.4 %line_11.1 = bf16[4,512,64]{2,1,0:T(8,128)(2,1)} custom-call(bf16[4,512,64]{2,1,0:T(8,128)(2,1)} %bitcast.165), custom_call_target="tpu_custom_call" | custom-call | tf_op jit(solution)/shard_map/line_11/pallas_call | solution.py:139
  443.9 4.0 collective-permute-start.6
  448.0 3.2 convolution_convert_fusion.2
  451.3 16.8 %scatter8_7.1 = f32[128,1024]{1,0:T(8,128)} custom-call(bf16[8,128,1024]{2,1,0:T(8,128)(2,1)} %bitcast.159), custom_call_target="tpu_custom_call" | custom-call | tf_op jit(solution)/shard_map/scatter8_7/pallas_call | solution.py:197
  470.0 9.2 %gather8_13.1 = f32[8,17,128]{2,1,0:T(8,128)} custom-call(f32[17,128]{1,0:T(8,128)} %bitcast.185), custom_call_target="tpu_custom_call" | custom-call | tf_op jit(solution)/shard_map/gather8_13/pallas_call | solution.py:99
  480.7 6.4 %line_14.1 = f32[4,17,128]{2,1,0:T(8,128)} custom-call(f32[17,128]{1,0:T(8,128)} %reduce_sum.246.x_ref), custom_call_target="tpu_custom_call" | custom-call | tf_op jit(solution)/shard_map/line_14/pallas_call | solution.py:139
  489.2 2.4 fusion.31
  491.6 2.4 copy.170
  493.9 29.0 %line_9.1 = bf16[4,576,256]{2,1,0:T(8,128)(2,1)} custom-call(bf16[4,576,256]{2,1,0:T(8,128)(2,1)} %bitcast.154), custom_call_target="tpu_custom_call" | custom-call | tf_op jit(solution)/shard_map/line_9/pallas_call | solution.py:139
  527.6 17.1 %swap8_10.1 = f32[8,288,64]{2,1,0:T(8,128)} custom-call(f32[8,288,64]{2,1,0:T(8,128)} %bitcast.156), custom_call_target="tpu_custom_call" | custom-call | tf_op jit(solution)/shard_map/swap8_10/pallas_call | solution.py:241
  544.7 2.1 copy.156
  546.8 2.1 reshape.523
  (234 shorter events, 63.1 us)
Async XLA Ops:
  0.6 6.3 %copy-start.12 = (f32[512,1024]{1,0:T(8,128)S(1)}, f32[512,1024]{1,0:T(8,128)}, u32[]{:S(2)}) copy-start(f32[512,1024]{1,0:T(8,128)} %param.23) | copy-start | bytes 6291460
  5.5 110.4 %collective-permute-start = (bf16[512,256]{1,0:T(8,128)(2,1)}, bf16[512,256]{1,0:T(8,128)(2,1)}, u32[]{:S(2)}, u32[]{:S(2)}) collective-permute-start(bf16[512,256]{1,0:T(8,128)(2,1)} %pad_maximum_fusion.7), channel_id=1, source_target_pairs={{0,1},{1,0},{2,3},{3,2},{4,5},{5,4},{6,7},{7,6},{8,9},{9,8},{10,11... | collective-permute-start | bytes 786440 | tf_op jit(solution)/shard_map/ppermute | solution.py:474
  6.7 108.0 %collective-permute-start.1 = (s32[1,8]{1,0:T(1,128)}, s32[1,8]{1,0:T(1,128)S(1)}, u32[]{:S(2)}, u32[]{:S(2)}) collective-permute-start(s32[1,8]{1,0:T(1,128)} %param.15), channel_id=1, source_target_pairs={{0,1},{1,0},{2,3},{3,2},{4,5},{5,4},{6,7},{7,6},{8,9},{9,8},{10,11... | collective-permute-start | bytes 104 | tf_op jit(solution)/shard_map/ppermute | solution.py:481
  8.1 176.5 %collective-permute-start.2 = (bf16[512,1024]{1,0:T(8,128)(2,1)}, bf16[512,1024]{1,0:T(8,128)(2,1)}, u32[]{:S(2)}, u32[]{:S(2)}) collective-permute-start(bf16[512,1024]{1,0:T(8,128)(2,1)} %convert_element_type.113), channel_id=1, source_target_pairs={{0,1},{1,0},{2,3},{3,2},{4,5},{5,4},{6,7},{7,6},{8,9},{9,8},{10,11... | collective-permute-start | bytes 3145736 | tf_op jit(solution)/shard_map/ppermute | solution.py:477
  20.3 4.9 copy-start.9
  20.3 171.7 %collective-permute-start.4 = (bf16[512,1152]{1,0:T(8,128)(2,1)}, bf16[512,1152]{1,0:T(8,128)(2,1)}, u32[]{:S(2)}, u32[]{:S(2)}) collective-permute-start(bf16[512,1152]{1,0:T(8,128)(2,1)} %concatenate.123), channel_id=1, source_target_pairs={{0,1},{1,0},{2,3},{3,2},{4,5},{5,4},{6,7},{7,6},{8,9},{9,8},{10,11... | collective-permute-start | bytes 3538952 | tf_op jit(solution)/shard_map/ppermute | solution.py:478
  23.9 173.3 %collective-permute-start.3 = (bf16[288,1024]{1,0:T(8,128)(2,1)}, bf16[288,1024]{1,0:T(8,128)(2,1)}, u32[]{:S(2)}, u32[]{:S(2)}) collective-permute-start(bf16[288,1024]{1,0:T(8,128)(2,1)} %pad_maximum_fusion.4), channel_id=1, source_target_pairs={{0,1},{1,0},{2,3},{3,2},{4,5},{5,4},{6,7},{7,6},{8,9},{9,8},{10,11... | collective-permute-start | bytes 1769480 | tf_op jit(solution)/shard_map/ppermute | solution.py:479
  25.2 90.1 %copy-start.46 = (f32[32]{0:T(128)}, f32[32]{0:T(128)S(1)}, u32[]{:S(2)}) copy-start(f32[32]{0:T(128)S(1)} %multiply_power_fusion) | copy-start | bytes 388
  102.1 6.8 %copy-start.42 = (f32[1024]{0:T(1024)S(1)}, f32[1024]{0:T(1024)}, u32[]{:S(2)}) copy-start(f32[1024]{0:T(1024)} %param.16) | copy-start | bytes 12292
  107.1 7.6 %copy-start.55 = (f32[128]{0:T(128)}, f32[128]{0:T(128)S(1)}, u32[]{:S(2)}) copy-start(f32[128]{0:T(128)S(1)} %fusion.32) | copy-start | bytes 1540
  115.1 5.6 %copy-start.34 = (f32[1024]{0:T(1024)}, f32[1024]{0:T(1024)S(1)}, u32[]{:S(2)}) copy-start(f32[1024]{0:T(1024)S(1)} %fusion.48) | copy-start | bytes 12292
  115.9 38.2 %copy-start.19 = (f32[1024,32]{0,1:T(8,128)}, f32[1024,32]{0,1:T(8,128)S(1)}, u32[]{:S(2)}) copy-start(f32[1024,32]{0,1:T(8,128)S(1)} %get-tuple-element.126) | copy-start | bytes 393220
  118.6 34.6 %copy-start.5 = (f32[1024,256]{0,1:T(8,128)}, f32[1024,256]{0,1:T(8,128)S(1)}, u32[]{:S(2)}) copy-start(f32[1024,256]{0,1:T(8,128)S(1)} %fusion.63) | copy-start | bytes 3145732
  118.9 7.7 %copy-start.2 = (f32[1024,64]{1,0:T(8,128)}, f32[1024,64]{1,0:T(8,128)S(1)}, u32[]{:S(2)}) copy-start(f32[1024,64]{1,0:T(8,128)S(1)} %copy.161) | copy-start | bytes 786436
  119.8 6.8 %copy-start.36 = (f32[1024]{0:T(1024)}, f32[1024]{0:T(1024)S(1)}, u32[]{:S(2)}) copy-start(f32[1024]{0:T(1024)S(1)} %fusion.49) | copy-start | bytes 12292
  184.6 7.4 %copy-start.18 = (bf16[512,1152]{1,0:T(8,128)(2,1)S(1)}, bf16[512,1152]{1,0:T(8,128)(2,1)}, u32[]{:S(2)}) copy-start(bf16[512,1152]{1,0:T(8,128)(2,1)} %concatenate.122) | copy-start | bytes 3538948
  184.6 7.4 %copy-start.38 = (f32[1024]{0:T(1024)S(1)}, f32[1024]{0:T(1024)}, u32[]{:S(2)}) copy-start(f32[1024]{0:T(1024)} %param.19) | copy-start | bytes 12292
  191.1 9.8 %copy-start.20 = (f32[1024,1024]{1,0:T(8,128)}, f32[1024,1024]{1,0:T(8,128)S(1)}, u32[]{:S(2)}) copy-start(f32[1024,1024]{1,0:T(8,128)S(1)} %get-tuple-element.128) | copy-start | bytes 12582916
  191.9 5.3 copy-start.15
  191.9 5.3 copy-start.22
  192.0 5.3 copy-start.23
  200.8 9.0 %copy-start.58 = (bf16[1024,576]{0,1:T(8,128)(2,1)}, bf16[1024,576]{0,1:T(8,128)(2,1)S(1)}, u32[]{:S(2)}) copy-start(bf16[1024,576]{0,1:T(8,128)(2,1)S(1)} %get-tuple-element.92) | copy-start | bytes 3538948
  334.2 5.5 copy-start.3
  334.2 5.5 copy-start.37
  334.3 5.5 copy-start.48
  343.0 16.0 %copy-start.16 = (bf16[8,1,128,1024]{3,2,1,0:T(8,128)(2,1)S(1)}, bf16[8,1,128,1024]{3,2,1,0:T(8,128)(2,1)}, u32[]{:S(2)}) copy-start(bf16[8,1,128,1024]{3,2,1,0:T(8,128)(2,1)} %get-tuple-element.93) | copy-start | bytes 6291460
  420.5 130.7 %collective-permute-start.7 = (f32[2,144,512]{2,1,0:T(8,128)}, f32[2,144,512]{2,1,0:T(8,128)}, u32[]{:S(2)}, u32[]{:S(2)}) collective-permute-start(f32[2,144,512]{2,1,0:T(8,128)} %get-tuple-element.100), channel_id=1, source_target_pairs={{0,1},{1,0},{2,3},{3,2},{4,5},{5,4},{6,7},{7,6},{8,9},{9,8},{10,11... | collective-permute-start | bytes 1769480 | tf_op jit(solution)/shard_map/ppermute | solution.py:573
  424.2 17.4 %slice-start.1 = ((f32[256,256]{1,0:T(8,128)}), f32[256,128]{1,0:T(8,128)S(1)}, s32[]{:S(2)}) async-start(f32[256,256]{1,0:T(8,128)} %copy-done.17), calls=%async_computation.1 | async-start | bytes 262144 | tf_op jit(solution)/shard_map/slice | solution.py:595
  427.0 20.9 %copy-start.25 = (bf16[1024,2,64]{0,2,1:T(8,128)(2,1)S(1)}, bf16[1024,2,64]{0,2,1:T(8,128)(2,1)}, u32[]{:S(2)}) copy-start(bf16[1024,2,64]{0,2,1:T(8,128)(2,1)} %fusion.28) | copy-start | bytes 786436
  427.0 20.9 %copy-start.27 = (bf16[512,64]{1,0:T(8,128)(2,1)S(1)}, bf16[512,64]{1,0:T(8,128)(2,1)}, u32[]{:S(2)}) copy-start(bf16[512,64]{1,0:T(8,128)(2,1)} %get-tuple-element.105) | copy-start | bytes 196612
  427.0 20.9 %copy-start.28 = (bf16[512,64]{1,0:T(8,128)(2,1)S(1)}, bf16[512,64]{1,0:T(8,128)(2,1)}, u32[]{:S(2)}) copy-start(bf16[512,64]{1,0:T(8,128)(2,1)} %get-tuple-element.130) | copy-start | bytes 196612
  427.0 20.9 %copy-start.30 = (bf16[1024,64]{0,1:T(8,128)(2,1)S(1)}, bf16[1024,64]{0,1:T(8,128)(2,1)}, u32[]{:S(2)}) copy-start(bf16[1024,64]{0,1:T(8,128)(2,1)} %copy-done.29) | copy-start | bytes 393220
  427.1 20.9 %copy-start.32 = (bf16[1024,64]{0,1:T(8,128)(2,1)S(1)}, bf16[1024,64]{0,1:T(8,128)(2,1)}, u32[]{:S(2)}) copy-start(bf16[1024,64]{0,1:T(8,128)(2,1)} %copy-done.31) | copy-start | bytes 393220
  427.1 20.9 %copy-start.33 = (bf16[512,128]{1,0:T(8,128)(2,1)S(1)}, bf16[512,128]{1,0:T(8,128)(2,1)}, u32[]{:S(2)}) copy-start(bf16[512,128]{1,0:T(8,128)(2,1)} %get-tuple-element.95) | copy-start | bytes 393220
  441.9 107.0 %collective-permute-start.5 = (f32[256,128]{1,0:T(8,128)S(1)}, f32[256,128]{1,0:T(8,128)S(1)}, u32[]{:S(2)}, u32[]{:S(2)}) collective-permute-start(f32[256,128]{1,0:T(8,128)S(1)} %bitcast.181), channel_id=1, source_target_pairs={{0,0},{1,16},{2,4},{3,20},{4,8},{5,24},{6,12},{7,28},{8,2},{9,18},... | collective-permute-start | bytes 393224 | tf_op jit(solution)/shard_map/ppermute | solution.py:610
  443.9 105.0 %collective-permute-start.6 = (f32[256,128]{1,0:T(8,128)S(1)}, f32[256,128]{1,0:T(8,128)S(1)}, u32[]{:S(2)}, u32[]{:S(2)}) collective-permute-start(f32[256,128]{1,0:T(8,128)S(1)} %bitcast.182), channel_id=1, source_target_pairs={{0,2},{1,18},{2,6},{3,22},{4,10},{5,26},{6,14},{7,30},{8,0},{9,16}... | collective-permute-start | bytes 393224 | tf_op jit(solution)/shard_map/ppermute | solution.py:610
  451.2 16.8 %copy-start.43 = (f32[1024]{0:T(1024)S(1)}, f32[1024]{0:T(1024)}, u32[]{:S(2)}) copy-start(f32[1024]{0:T(1024)} %param.16) | copy-start | bytes 12292
  451.2 16.9 %copy-start.51 = (f32[128]{0:T(128)S(1)}, f32[128]{0:T(128)}, u32[]{:S(2)}) copy-start(f32[128]{0:T(128)} %fusion.54) | copy-start | bytes 1540
  451.2 18.1 %copy-start.44 = (f32[1024]{0:T(1024)S(1)}, f32[1024]{0:T(1024)}, u32[]{:S(2)}) copy-start(f32[1024]{0:T(1024)} %get-tuple-element.60) | copy-start | bytes 12292
  451.2 18.1 %copy-start.52 = (f32[64]{0:T(128)S(1)}, f32[64]{0:T(128)}, u32[]{:S(2)}) copy-start(f32[64]{0:T(128)} %get-tuple-element.66) | copy-start | bytes 772
  451.2 37.9 %copy-start.56 = (f32[128]{0:T(128)S(1)}, f32[128]{0:T(128)}, u32[]{:S(2)}) copy-start(f32[128]{0:T(128)} %copy-done.55) | copy-start | bytes 1540
  451.2 37.9 %copy-start.4 = (f32[2,128,1024]{2,1,0:T(8,128)S(1)}, f32[2,128,1024]{2,1,0:T(8,128)}, u32[]{:S(2)}) copy-start(f32[2,128,1024]{2,1,0:T(8,128)} %scatter8_4.1) | copy-start | bytes 3145732
  451.2 37.9 %copy-start.10 = (bf16[1,128,1024]{2,1,0:T(8,128)(2,1)S(1)}, bf16[1,128,1024]{2,1,0:T(8,128)(2,1)}, u32[]{:S(2)}) copy-start(bf16[1,128,1024]{2,1,0:T(8,128)(2,1)} %param.27) | copy-start | bytes 786436
  451.3 37.9 %copy-start.39 = (f32[1024]{0:T(1024)S(1)}, f32[1024]{0:T(1024)}, u32[]{:S(2)}) copy-start(f32[1024]{0:T(1024)} %param.19) | copy-start | bytes 12292
  451.3 37.9 %copy-start.45 = (f32[128]{0:T(128)S(1)}, f32[128]{0:T(128)}, u32[]{:S(2)}) copy-start(f32[128]{0:T(128)} %fusion.53) | copy-start | bytes 1540
  451.3 37.9 %copy-start.50 = (f32[128]{0:T(128)S(1)}, f32[128]{0:T(128)}, u32[]{:S(2)}) copy-start(f32[128]{0:T(128)} %copy-done.49) | copy-start | bytes 1540
  493.9 30.5 %copy-start.14 = (bf16[4,512,64]{2,1,0:T(8,128)(2,1)S(1)}, bf16[4,512,64]{2,1,0:T(8,128)(2,1)}, u32[]{:S(2)}) copy-start(bf16[4,512,64]{2,1,0:T(8,128)(2,1)} %line_11.1) | copy-start | bytes 786436
  544.7 5.1 copy-start.54
  (21 other events, 56.5 us)

commit v2 on v1

v2 whole, which is shorter than its diff:
```python
import functools

import jax
import jax.numpy as jnp
from jax import lax
from jax.experimental import pallas as pl
from jax.experimental.pallas import tpu as pltpu
from jax.sharding import PartitionSpec as P

QUERY_HEADS = 16
KEY_VALUE_HEADS = 8
HEAD_SIZE = 64
FF = 4608
WIDTH = 1024
ROWS = 128

epsilon = 1e-05
rope_base = 1000000.0
MESH = pl.DeviceIdType.MESH
ANY = pl.ANY
bf16 = jnp.bfloat16
f32 = jnp.float32


def who():
    n = lax.axis_size("ctx")
    c = lax.axis_index("ctx")
    f = lax.axis_index("fsdp")
    q = n // 4
    return c // q, (c % q) // 2, c % 2, f


def dev(z, m, core, f):
    return (z * (lax.axis_size("ctx") // 4) + m * 2 + core, f)


def slot(z, core):
    return z * 2 + core


def enter(peers):
    bar = pltpu.get_barrier_semaphore()
    for p in peers:
        pl.semaphore_signal(bar, inc=1, device_id=p, device_id_type=MESH)
    pl.semaphore_wait(bar, len(peers))


def rcopy(src, dst, s, r, to):
    return pltpu.make_async_remote_copy(
        src_ref=src, dst_ref=dst, send_sem=s, recv_sem=r, device_id=to, device_id_type=MESH
    )


def comm_params(cid):
    return pltpu.CompilerParams(collective_id=cid, has_side_effects=True)


def any_specs(n):
    return [pl.BlockSpec(memory_space=ANY)] * n


def gather8_kernel(x_ref, o_ref, ss, rs, ls):
    z, m, core, f = who()
    sib = dev(z, m, 1 - core, f)
    peers = [dev((z + s) % 4, m, core, f) for s in (1, 2, 3)]
    me = slot(z, core)
    own = pltpu.make_async_copy(x_ref, o_ref.at[me], ls)
    own.start()
    enter([sib] + peers)
    first = []
    for k in (1, 0, 2):
        cp = rcopy(x_ref, o_ref.at[me], ss.at[k], rs.at[k], peers[k])
        cp.start()
        first.append((k, cp))
    cp0 = rcopy(x_ref, o_ref.at[me], ss.at[3], rs.at[3], sib)
    cp0.start()
    fw = []
    for k, cp in first:
        sl = slot((z + 3 - k) % 4, core)
        cp.wait_recv()
        cp = rcopy(o_ref.at[sl], o_ref.at[sl], ss.at[4 + k], rs.at[4 + k], sib)
        cp.start()
        fw.append(cp)
    for cp in fw + [cp0]:
        cp.wait_recv()
    for cp in [cp for _, cp in first] + [cp0] + fw:
        cp.wait_send()
    own.wait()


def gather8(x, cid):
    return pl.pallas_call(
        gather8_kernel,
        out_shape=jax.ShapeDtypeStruct((8,) + x.shape, x.dtype),
        in_specs=any_specs(1),
        out_specs=any_specs(1)[0],
        scratch_shapes=[
            pltpu.SemaphoreType.DMA((7,)),
            pltpu.SemaphoreType.DMA((7,)),
            pltpu.SemaphoreType.DMA,
        ],
        compiler_params=comm_params(cid),
        name="gather8_%d" % cid,
    )(x)


def across_kernel(both, same, x_ref, o_ref, ss, rs, ls):
    z, m, core, f = who()
    M = lax.axis_size("ctx") // 8
    count = M * 2 if both else M
    me = m * 2 + f if both else m
    others = [(me + s) % count for s in range(1, count)]
    peers = [dev(z, o // 2, core, o % 2) if both else dev(z, o, core, f) for o in others]

    def src(k):
        return x_ref if same else x_ref.at[k]

    own = pltpu.make_async_copy(src(me), o_ref.at[me], ls)
    own.start()
    enter(peers)
    cps = []
    for s in range(count - 1):
        cp = rcopy(src(others[s]), o_ref.at[me], ss.at[s], rs.at[s], peers[s])
        cp.start()
        cps.append(cp)
    for cp in cps:
        cp.wait_recv()
    for cp in cps:
        cp.wait_send()
    own.wait()


def across(x, both, same, cid):
    shp = x.shape if same else x.shape[1:]
    count = lax.axis_size("ctx") // (4 if both else 8)
    return pl.pallas_call(
        functools.partial(across_kernel, both, same),
        out_shape=jax.ShapeDtypeStruct((count,) + shp, x.dtype),
        in_specs=any_specs(1),
        out_specs=any_specs(1)[0],
        scratch_shapes=[
            pltpu.SemaphoreType.DMA((count - 1,)),
            pltpu.SemaphoreType.DMA((count - 1,)),
            pltpu.SemaphoreType.DMA,
        ],
        compiler_params=comm_params(cid),
        name="across_%d" % cid,
    )(x)


def scatter8_kernel(x_ref, o_ref, a, b, s_buf, d, ls, s1, r1, s2, r2):
    z, m, core, f = who()
    sib = dev(z, m, 1 - core, f)
    to = [(z + s) % 4 for s in (1, 2, 3, 0)]
    peers = [dev(zz, m, core, f) for zz in to[:3]]
    loads = []
    for k in range(4):
        cp = pltpu.make_async_copy(x_ref.at[slot(to[k], core)], a.at[k], ls.at[k])
        cp.start()
        loads.append(cp)
    enter([sib] + peers)
    ones = []
    for k in range(4):
        cp = rcopy(x_ref.at[slot(to[k], 1 - core)], b.at[k], s1.at[k], r1.at[k], sib)
        cp.start()
        ones.append(cp)
    twos = []
    for k in range(3):
        loads[k].wait()
        ones[k].wait_recv()
        s_buf[k] = (a[k].astype(f32) + b[k].astype(f32)).astype(s_buf.dtype)
        cp = rcopy(s_buf.at[k], d.at[k], s2.at[k], r2.at[k], peers[k])
        cp.start()
        twos.append(cp)
    loads[3].wait()
    ones[3].wait_recv()
    total = a[3].astype(f32) + b[3].astype(f32)
    for k in range(3):
        twos[k].wait_recv()
        total = total + d[k].astype(f32)
    o_ref[...] = total
    for cp in ones + twos:
        cp.wait_send()


def scatter8(x, cid):
    shp = x.shape[1:]
    return pl.pallas_call(
        scatter8_kernel,
        out_shape=jax.ShapeDtypeStruct(shp, f32),
        in_specs=any_specs(1),
        out_specs=pl.BlockSpec(memory_space=pltpu.VMEM),
        scratch_shapes=[
            pltpu.VMEM((4,) + shp, x.dtype),
            pltpu.VMEM((4,) + shp, x.dtype),
            pltpu.VMEM((3,) + shp, x.dtype),
            pltpu.VMEM((3,) + shp, x.dtype),
            pltpu.SemaphoreType.DMA((4,)),
            pltpu.SemaphoreType.DMA((4,)),
            pltpu.SemaphoreType.DMA((4,)),
            pltpu.SemaphoreType.DMA((3,)),
            pltpu.SemaphoreType.DMA((3,)),
        ],
        compiler_params=comm_params(cid),
        name="scatter8_%d" % cid,
    )(x)


def back_product(left, right):
    return lax.dot_general(
        left, right, (((1,), (1,)), ((), ())), preferred_element_type=f32
    )


def lead_sum(left, right):
    return lax.dot_general(
        left, right, (((0,), (0,)), ((), ())), preferred_element_type=f32
    )


def dot(left, right):
    return jnp.dot(left, right, preferred_element_type=f32)


BLOCK = 2 * ROWS


def block_weights(q, k, begin, z, m, mm, span):
    keys = (z + 1) * BLOCK
    key = lax.broadcasted_iota(jnp.int32, (1, keys), 1)
    key = key // BLOCK * span + key % BLOCK + mm * BLOCK
    token = z * span + m * BLOCK + lax.broadcasted_iota(jnp.int32, (BLOCK, 1), 0)
    e = jnp.exp(back_product(q, k))
    return jnp.where((key >= begin) & (key <= token), e, 0.0)


def attend_kernel(span, m_ref, q_ref, kv_ref, begin_ref, sum_ref, tot_ref):
    m = m_ref[0]
    for z in range(4):
        rows = slice(z * BLOCK, (z + 1) * BLOCK)
        keys = (z + 1) * BLOCK
        for h in range(2):
            lanes = slice(h * 64, h * 64 + 64)
            acc = jnp.zeros((BLOCK, 64), f32)
            tot = jnp.zeros((BLOCK, 1), f32)
            q = q_ref[rows, lanes]

            def step(mm, carry):
                acc, tot = carry
                e = block_weights(q, kv_ref[mm, :keys, :64], begin_ref[rows, :], z, m, mm, span)
                acc = acc + dot(e.astype(bf16), kv_ref[mm, :keys, 64:])
                return acc, tot + jnp.sum(e, axis=1, keepdims=True)

            acc, tot = lax.fori_loop(0, kv_ref.shape[0], step, (acc, tot))
            sum_ref[rows, lanes] = acc
            tot_ref[rows, lanes] = jnp.broadcast_to(tot, (BLOCK, 64))


VM = pltpu.VMEM


def vspecs(n):
    return [pl.BlockSpec(memory_space=VM)] * n


def attend(m, q, kv, begin, span):
    n = q.shape[0]
    return pl.pallas_call(
        functools.partial(attend_kernel, span),
        out_shape=(jax.ShapeDtypeStruct((n, 128), f32), jax.ShapeDtypeStruct((n, 128), f32)),
        in_specs=[pl.BlockSpec(memory_space=pltpu.SMEM)] + vspecs(3),
        out_specs=tuple(vspecs(2)),
        cost_estimate=pl.CostEstimate(flops=2**31, bytes_accessed=2**22, transcendentals=2**22),
        compiler_params=pltpu.CompilerParams(vmem_limit_bytes=40 * 2**20),
        name="attend",
    )(m, q, kv, begin)


def attend_back_kernel(span, m_ref, q_ref, kv_ref, begin_ref, g_ref, delta_ref, dq_ref, dkv_ref, acc_ref):
    m = m_ref[0]
    dq_ref[...] = jnp.zeros_like(dq_ref)

    def step(mm, _):
        acc_ref[...] = jnp.zeros_like(acc_ref)
        for z in range(4):
            rows = slice(z * BLOCK, (z + 1) * BLOCK)
            keys = (z + 1) * BLOCK
            for h in range(2):
                lanes = slice(h * 64, h * 64 + 64)
                q = q_ref[rows, lanes]
                g = g_ref[rows, lanes]
                k = kv_ref[mm, :keys, :64]
                v = kv_ref[mm, :keys, 64:]
                e = block_weights(q, k, begin_ref[rows, :], z, m, mm, span)
                dp = back_product(g, v)
                ds = (e * (dp - delta_ref[rows, h * 64 : h * 64 + 1])).astype(bf16)
                dq_ref[rows, lanes] += dot(ds, k)
                acc_ref[:keys, :64] += lead_sum(ds, q)
                acc_ref[:keys, 64:] += lead_sum(e.astype(bf16), g)
        dkv_ref[mm] = acc_ref[...].astype(dkv_ref.dtype)
        return 0

    lax.fori_loop(0, kv_ref.shape[0], step, 0)


def attend_back(m, q, kv, begin, g, delta, span):
    n = q.shape[0]
    return pl.pallas_call(
        functools.partial(attend_back_kernel, span),
        out_shape=(jax.ShapeDtypeStruct((n, 128), f32), jax.ShapeDtypeStruct(kv.shape, bf16)),
        in_specs=[pl.BlockSpec(memory_space=pltpu.SMEM)] + vspecs(5),
        out_specs=tuple(vspecs(2)),
        scratch_shapes=[pltpu.VMEM((n, 128), f32)],
        cost_estimate=pl.CostEstimate(flops=2**33, bytes_accessed=2**23, transcendentals=2**22),
        compiler_params=pltpu.CompilerParams(vmem_limit_bytes=48 * 2**20),
        name="attend_back",
    )(m, q, kv, begin, g, delta)


def root_mean_norm(rows, gain):
    return (
        rows * lax.rsqrt(jnp.mean(rows * rows, axis=-1, keepdims=True) + epsilon) * gain
    )


def rotary(rows, cosine, sine):
    halfway = rows.shape[-1] // 2
    leading = rows[..., :halfway]
    trailing = rows[..., halfway:]
    return jnp.concatenate(
        [leading * cosine - trailing * sine, leading * sine + trailing * cosine], axis=-1
    )


SWAP = [(0, 1), (1, 0)]


def halves(f, own, other, axis):
    return jnp.where(
        f == 0,
        jnp.concatenate([own, other], axis=axis),
        jnp.concatenate([other, own], axis=axis),
    )


def local(
    hidden_in,
    doc_lengths,
    attn_gain,
    query_gain,
    key_norm_gain,
    ffn_gain,
    query_proj,
    key_weight,
    value_weight,
    attn_proj,
    gate_proj,
    up_proj,
    down_proj,
    out_cotangent,
):
    n_ctx = lax.axis_size("ctx")
    M = n_ctx // 8
    T = 2 * M
    z, m, core, f = who()
    head = slot(z, core)
    tokens = 8 * ROWS
    span = n_ctx // 4 * ROWS
    segment = FF // n_ctx
    columns = M * segment
    half_width = WIDTH // 2
    each = WIDTH // n_ctx

    heads_own = jnp.concatenate(
        [
            lax.dynamic_slice(query_proj, (0, head * 128), (half_width, 128)),
            lax.dynamic_slice(key_weight, (0, head * 64), (half_width, 64)),
            lax.dynamic_slice(value_weight, (0, head * 64), (half_width, 64)),
        ],
        axis=1,
    ).astype(bf16)
    first = z * (n_ctx // 4) + core
    glu_own = jnp.concatenate(
        [
            lax.dynamic_slice(w, (0, (first + 2 * mm) * segment), (half_width, segment)).astype(bf16)
            for w in (gate_proj, up_proj)
            for mm in range(M)
        ],
        axis=1,
    )
    down_own = jnp.concatenate(
        [
            lax.dynamic_slice(
                down_proj, ((first + 2 * mm) * segment - f * (FF // 2), 0), (segment, WIDTH)
            )
            for mm in range(M)
        ],
        axis=0,
    ).astype(bf16)
    out_own = attn_proj.astype(bf16)

    def swap(v):
        return lax.ppermute(v, "fsdp", SWAP)

    w_heads = halves(f, heads_own, swap(heads_own), 0)
    x_all = gather8(hidden_in[0], 1).reshape(tokens, WIDTH).astype(f32)
    heads_own, glu_own, down_own, out_own, cotangent, x_all = lax.optimization_barrier(
        (heads_own, glu_own, down_own, out_own, out_cotangent[0], x_all)
    )
    w_out = halves(f, out_own, swap(out_own), 0)
    w_glu = halves(f, glu_own, swap(glu_own), 0)
    w_down = jnp.where(f == z // 2, down_own, swap(down_own))

    starts = jnp.cumsum(doc_lengths[0]) - doc_lengths[0]
    token_index = (
        jnp.arange(4, dtype=jnp.int32)[:, None] * span
        + m * BLOCK
        + jnp.arange(BLOCK, dtype=jnp.int32)[None, :]
    ).reshape(tokens, 1)
    after = token_index >= starts[None, :]
    begins = jnp.max(jnp.where(after, starts[None, :], 0), axis=1, keepdims=True)
    place = token_index - begins
    freqs = rope_base ** (-2.0 * jnp.arange(32, dtype=f32) / 64)
    angles = place.astype(f32) * freqs[None, :]
    cosine = jnp.cos(angles)[:, None, :]
    sine = jnp.sin(angles)[:, None, :]

    normed = root_mean_norm(x_all, attn_gain).astype(bf16)
    stacked = dot(normed, w_heads)

    def rotate(q_in, k_in, q_gain, k_gain):
        q_out = (
            rotary(root_mean_norm(q_in.reshape(tokens, 2, HEAD_SIZE), q_gain), cosine, sine)
            * HEAD_SIZE ** (-0.5)
        )
        k_out = rotary(root_mean_norm(k_in.reshape(tokens, 1, HEAD_SIZE), k_gain), cosine, sine)
        return q_out.reshape(tokens, 128), k_out.reshape(tokens, 64)

    (q_rot, k_rot), heads_back = jax.vjp(
        rotate, stacked[:, :128], stacked[:, 128:192], query_gain, key_norm_gain
    )
    q_rows = q_rot.astype(bf16)
    kv_rows = jnp.concatenate([k_rot, stacked[:, 192:]], axis=1).astype(bf16)
    kv_all = across(kv_rows, False, True, 2)
    m_arr = jnp.full((1,), m, jnp.int32)
    summed, totals = attend(m_arr, q_rows, kv_all, begins, span)
    attended = gather8((summed / totals).astype(bf16), 3)
    attended = jnp.transpose(attended, (1, 0, 2)).reshape(tokens, WIDTH)
    c_all = gather8(cotangent, 15).reshape(tokens, WIDTH)
    middle = x_all + dot(attended, w_out)
    normed_ffn = root_mean_norm(middle, ffn_gain).astype(bf16)
    glu = dot(normed_ffn, w_glu)
    gate = glu[:, :columns]
    up = glu[:, columns:]
    sig = 1.0 / (1.0 + jnp.exp(-gate))
    silu = gate * sig
    hidden = (silu * up).astype(bf16)
    grad_hidden = back_product(c_all, w_down)
    grad_gate = (grad_hidden * up * (sig * (1.0 + gate * (1.0 - sig)))).astype(bf16)
    grad_up = (grad_hidden * silu).astype(bf16)
    grad_glu = jnp.concatenate([grad_gate, grad_up], axis=1)
    part_in = back_product(grad_glu, w_glu)
    part_out = dot(hidden, w_down)
    parts = jnp.stack(
        [part_in.reshape(8, ROWS, WIDTH), part_out.reshape(8, ROWS, WIDTH)], axis=1
    ).astype(bf16)
    own_sums = scatter8(parts, 4)

    own = lax.dynamic_slice(middle, (head * ROWS, 0), (ROWS, WIDTH))
    output = own + own_sums[1]
    _, ffn_back = jax.vjp(root_mean_norm, own, ffn_gain)
    grad_mid_norm, ffn_gain_part = ffn_back(own_sums[0])
    grad_middle = out_cotangent[0].astype(f32) + grad_mid_norm
    branch = gather8(grad_middle.astype(bf16), 5).reshape(tokens, WIDTH)

    w_out_head = lax.dynamic_slice(w_out, (head * 128, 0), (128, WIDTH))
    grad_mixed = back_product(branch, w_out_head)
    grad_summed = (grad_mixed / totals).astype(bf16)
    weighted = (grad_mixed * summed / (totals * totals)).reshape(tokens, 2, 64)
    delta = jnp.broadcast_to(
        jnp.sum(weighted, axis=2, keepdims=True), (tokens, 2, 64)
    ).reshape(tokens, 128)
    grad_q, dkv = attend_back(m_arr, q_rows, kv_all, begins, grad_summed, delta, span)
    dkv = jnp.sum(across(dkv, False, False, 6).astype(f32), axis=0)
    gq_pre, gk_pre, q_gain_part, k_gain_part = heads_back((grad_q, dkv[:, :64]))
    grad_stacked = jnp.concatenate([gq_pre, gk_pre, dkv[:, 64:]], axis=1).astype(bf16)
    part_normed = back_product(grad_stacked, w_heads).reshape(8, ROWS, WIDTH).astype(bf16)
    grad_normed = scatter8(part_normed, 7)
    _, attn_back = jax.vjp(root_mean_norm, hidden_in[0].astype(f32), attn_gain)
    grad_resid, attn_gain_part = attn_back(grad_normed)
    input_grad = grad_middle + grad_resid

    glu_part = lead_sum(grad_glu, normed_ffn).astype(bf16)
    glu_part = jnp.transpose(
        glu_part.reshape(2, M, segment, 2, half_width), (1, 3, 0, 2, 4)
    ).reshape(T, 2, segment, half_width)
    down_part = lead_sum(hidden, c_all).astype(bf16)
    down_part = jnp.transpose(
        down_part.reshape(columns, 2, 2, M, 2, each), (3, 1, 0, 2, 4, 5)
    ).reshape(T, columns, 4 * each)
    glu_grad = jnp.sum(across(glu_part, True, False, 8).astype(f32), axis=0)
    down_sum = jnp.sum(across(down_part, True, False, 9).astype(f32), axis=0)
    gate_grad = jnp.transpose(glu_grad[0])
    up_grad = jnp.transpose(glu_grad[1])

    devices = [
        (zz, mm, cc, ff) for zz in range(4) for mm in range(M) for cc in range(2) for ff in range(2)
    ]

    def number(zz, mm, cc, ff):
        return (zz * (n_ctx // 4) + mm * 2 + cc) * 2 + ff

    down_pieces = down_sum.reshape(columns, 2, 2, each)
    got = [[None, None], [None, None]]
    rounds = []
    for dz in range(2):
        for dc in range(2):
            piece = lax.dynamic_slice(
                down_pieces, (0, (z + dz) % 2, (core + dc) % 2, 0), (columns, 1, 1, each)
            ).reshape(columns, each)
            perm = [
                (number(zz, mm, cc, ff), number(2 * ff + (zz + dz) % 2, mm, (cc + dc) % 2, zz // 2))
                for zz, mm, cc, ff in devices
            ]
            rounds.append(lax.ppermute(piece, ("ctx", "fsdp"), perm))
    rounds = jnp.stack(rounds).reshape(2, 2, columns, each)
    rounds = jnp.where(z % 2 == 0, rounds, rounds[::-1])
    rounds = jnp.where(core == 0, rounds, rounds[:, ::-1])
    down_grad = jnp.transpose(
        rounds.reshape(2, 2, M, segment, each), (0, 2, 1, 3, 4)
    ).reshape(FF // 2, each)

    branch_columns = lax.dynamic_slice(
        branch.reshape(tokens, 4, M, 2, each), (0, z, 0, core, 0), (tokens, 1, M, 1, each)
    ).reshape(tokens, M * each)
    attn_part = lead_sum(attended, branch_columns).astype(bf16)
    attn_part = jnp.transpose(
        attn_part.reshape(2, half_width, M, each), (2, 0, 1, 3)
    ).reshape(T, half_width, each)
    attn_grad = jnp.sum(across(attn_part, True, False, 11).astype(f32), axis=0)

    heads_part = lead_sum(normed, grad_stacked).astype(bf16)
    qw, kw = 128 // M, 64 // M
    heads_part = jnp.concatenate(
        [
            heads_part[:, :128].reshape(2, half_width, M, qw),
            heads_part[:, 128:192].reshape(2, half_width, M, kw),
            heads_part[:, 192:].reshape(2, half_width, M, kw),
        ],
        axis=3,
    )
    heads_part = jnp.transpose(heads_part, (2, 0, 1, 3)).reshape(T, half_width, 256 // M)
    heads_grad = jnp.sum(across(heads_part, True, False, 12).astype(f32), axis=0)
    perm = [
        (number(zz, mm, cc, ff), number(zz, (cc * M + mm) // 2, (cc * M + mm) % 2, ff))
        for zz, mm, cc, ff in devices
    ]
    heads_grad = lax.ppermute(heads_grad, ("ctx", "fsdp"), perm)
    query_grad = heads_grad[:, :qw]
    key_grad = heads_grad[:, qw : qw + kw]
    value_grad = heads_grad[:, qw + kw :]

    gains = jnp.concatenate([attn_gain_part, ffn_gain_part, q_gain_part, k_gain_part])
    gains = jnp.sum(gather8(gains.reshape(17, 128), 13), axis=0)
    gains = jnp.sum(across(gains, True, True, 14), axis=0).reshape(-1)
    return (
        output[None],
        input_grad[None],
        gains[:WIDTH],
        gains[2 * WIDTH : 2 * WIDTH + 64],
        gains[2 * WIDTH + 64 :],
        gains[WIDTH : 2 * WIDTH],
        query_grad,
        key_grad,
        value_grad,
        attn_grad,
        gate_grad,
        up_grad,
        down_grad,
    )


def solution(mesh):
    in_specs = (
        P("fsdp", "ctx", None),
        P("fsdp", None),
        P(),
        P(),
        P(),
        P(),
        P("fsdp", None),
        P("fsdp", None),
        P("fsdp", None),
        P("fsdp", None),
        P("fsdp", None),
        P("fsdp", None),
        P("fsdp", None),
        P("fsdp", "ctx", None),
    )
    out_specs = (
        P("fsdp", "ctx", None),
        P("fsdp", "ctx", None),
        P(),
        P(),
        P(),
        P(),
        P("fsdp", "ctx"),
        P("fsdp", "ctx"),
        P("fsdp", "ctx"),
        P("fsdp", "ctx"),
        P("fsdp", "ctx"),
        P("fsdp", "ctx"),
        P("fsdp", "ctx"),
    )
    return jax.shard_map(local, mesh=mesh, in_specs=in_specs, out_specs=out_specs, check_vma=False)
```

time: 565 us -> 492 us (0.87)
  the two profiles are of different devices: /device:TPU:9 before, /device:TPU:0 now
where the time goes in v2:
time: 492 us; the launch traced here: 482 us
  Pallas kernels  312 us (63%)
  local copies, waits for them, and re-layouts  60.1 us (12%)
  other arithmetic  49.1 us (10%)
  matrix products  44.1 us (9%)
  starting transfers between devices  14 us (3%)
    pallas_call x5, Pallas kernels, gather8(): pl.pallas_call(gather8_kernel, out_shape=jax.ShapeDtypeStruct((8,) + x.sh...  125 us
    pallas_call x7, Pallas kernels, across(): pl.pallas_call(functools.partial(across_kernel, both, same), out_shape=ja...  95.4 us
    pallas_call x2, Pallas kernels, scatter8(): pl.pallas_call(scatter8_kernel, out_shape=jax.ShapeDtypeStruct(shp, f32),...  73.1 us
    dot_general x4, matrix products, dot(): return jnp.dot(left, right, preferred_element_type=f32)  18.2 us
    dot_general x4, matrix products, back_product(): lax.dot_general(left, right, (((1,), (1,)), ((), ())), preferred_element_...  15.5 us
    dot_general x4, matrix products, lead_sum(): lax.dot_general(left, right, (((0,), (0,)), ((), ())), preferred_element_...  10.4 us
    reshape x2, local copies, waits for them, and re-layouts, local(): glu_part.reshape(2, M, segment, 2, half_width)  10.4 us
    pallas_call x1, Pallas kernels, attend_back(): pl.pallas_call(functools.partial(attend_back_kernel, span), out_shape=(ja...  10.2 us
  transfers between devices with their start and end apart: 9, of which 0 were waited for; matrix products, arithmetic and copies ran while one was open for 19% of the time, Pallas kernels for 41%

profile of v2, /device:TPU:0, one launch (start us, length us, event | category | flops | bytes accessed | tf_op | source)
XLA Modules:
  0.0 482.5 jit_solution(8361310329314541408)
XLA Ops:
  3.7 3.0 collective-permute-start
  6.7 24.7 %gather8_1.1 = bf16[8,128,1024]{2,1,0:T(8,128)(2,1)} custom-call(bf16[128,1024]{1,0:T(8,128)(2,1)} %bitcast.157), custom_call_target="tpu_custom_call" | custom-call | tf_op jit(solution)/shard_map/gather8_1/pallas_call | solution.py:92
  31.4 4.2 bitcast_convert_fusion
  39.7 2.8 dynamic-slice_convert_fusion.2
  42.5 2.8 concatenate.54
  48.0 2.5 multiply_reduce_fusion.1
  51.9 27.4 %gather8_15.1 = bf16[8,128,1024]{2,1,0:T(8,128)(2,1)} custom-call(bf16[128,1024]{1,0:T(8,128)(2,1)} %bitcast.161), custom_call_target="tpu_custom_call" | custom-call | tf_op jit(solution)/shard_map/gather8_15/pallas_call | solution.py:92
  80.0 3.3 fusion.46
  84.7 3.1 fusion.11
  89.0 9.1 %across_2.1.kv_ref = bf16[2,1024,128]{2,1,0:T(8,128)(2,1)} custom-call(bf16[1024,128]{1,0:T(8,128)(2,1)} %pad_maximum_fusion.9.x_ref), custom_call_target="tpu_custom_call" | custom-call | tf_op jit(solution)/shard_map/across_2/pallas_call | solution.py:136
  99.2 8.3 %attend.1 = (f32[1024,128]{1,0:T(8,128)S(1)}, f32[1024,128]{1,0:T(8,128)S(1)}) custom-call(s32[1]{0:T(128)} %bitcast.3.m_ref, bf16[1024,128]{1,0:T(8,128)(2,1)S(1)} %copy.167.q_ref, bf16[2,1024,128]{2,1,0:T(8,128)(2,1)S(1)} %copy-done.2, s32[1024,1]{1,0:T(8,128)S(1)} %copy.168.begin_ref), custom_call_target="tpu_custom_call" | custom-call | flops 2147483648 | bytes 4194304 | tf_op jit(solution)/shard_map/attend/pallas_call | solution.py:268
  108.3 27.7 %gather8_3.1 = bf16[8,1024,128]{2,1,0:T(8,128)(2,1)} custom-call(bf16[1024,128]{1,0:T(8,128)(2,1)} %divide_convert_fusion.1.x_ref), custom_call_target="tpu_custom_call" | custom-call | tf_op jit(solution)/shard_map/gather8_3/pallas_call | solution.py:92
  136.0 4.4 copy.169
  140.3 3.4 maximum_select_fusion.1
  143.8 5.1 %multiply_reduce_fusion = (f32[1024]{0:T(1024)S(1)}, f32[1024,1024]{1,0:T(8,128)S(1)}) fusion(f32[1024,1024]{1,0:T(8,128)S(1)} %copy-done.4, bf16[1024,1024]{0,1:T(8,128)(2,1)} %bitcast.151, bf16[1024,1024]{1,0:T(8,128)(2,1)S(1)} %maximum_select_fusion.1), kind=kOutput, calls=%fused_computation.4 | convolution fusion | flops 2150628352 | bytes 12587008 | tf_op jit(solution)/shard_map/dot_general | solution.py:222
  149.1 6.7 %fusion.31 = f32[1024,1152]{0,1:T(8,128)S(1)} fusion(bf16[512,1152]{1,0:T(8,128)(2,1)} %collective-permute-done.3, bf16[512,1152]{1,0:T(8,128)(2,1)} %concatenate.54, pred[]{:T(512)S(6)} %eq.26, f32[1024,1024]{1,0:T(8,128)S(1)} %get-tuple-element.116, f32[1024]{0:T(1024)S(1)} %copy-done.41, f32[1024]{0:T(1024)S(1)} %add_rsqrt_fusion), kind=kOutput, calls=%fused_computation.105 | convolution fusion | flops 2429681664 | bytes 11280385 | tf_op jit(solution)/shard_map/dot_general | solution.py:222
  155.9 3.5 multiply_convert_fusion.4
  159.4 2.4 convolution_convert_fusion.4
  161.8 4.2 convolution_convert_fusion
  166.0 5.6 %convolution_convert_fusion.1 = bf16[1024,1024]{1,0:T(8,128)(2,1)S(1)} fusion(bf16[1024,576]{0,1:T(8,128)(2,1)S(1)} %get-tuple-element.85, bf16[1024,576]{0,1:T(8,128)(2,1)S(1)} %get-tuple-element.84, bf16[512,1152]{1,0:T(8,128)(2,1)} %collective-permute-done.3, bf16[512,1152]{1,0:T(8,128)(2,1)} %concatenate.54, pred[]{:T(512)S(6)} %eq.26), kind=kOutput, calls=%fused_computation.19 | convolution fusion | flops 2432303104 | bytes 6815745 | tf_op jit(solution)/shard_map/dot_general | solution.py:210
  171.6 3.1 convolution_convert_fusion.3
  174.7 2.3 pad_maximum_fusion.x_ref
  177.1 45.6 %scatter8_4.1 = f32[2,128,1024]{2,1,0:T(8,128)} custom-call(bf16[8,2,128,1024]{3,2,1,0:T(8,128)(2,1)} %pad_maximum_fusion.x_ref), custom_call_target="tpu_custom_call" | custom-call | tf_op jit(solution)/shard_map/scatter8_4/pallas_call | solution.py:188
  222.7 1.9 fusion.28
  224.6 2.1 fusion.45.x_ref
  226.7 33.9 %gather8_5.1 = bf16[8,128,1024]{2,1,0:T(8,128)(2,1)} custom-call(bf16[128,1024]{1,0:T(8,128)(2,1)} %fusion.45.x_ref), custom_call_target="tpu_custom_call" | custom-call | tf_op jit(solution)/shard_map/gather8_5/pallas_call | solution.py:92
  260.6 4.2 copy.185
  264.8 3.1 multiply_divide_fusion
  271.2 10.2 %attend_back.1 = (f32[1024,128]{1,0:T(8,128)S(1)}, bf16[2,1024,128]{2,1,0:T(8,128)(2,1)S(1)}) custom-call(s32[1]{0:T(128)} %bitcast.3.m_ref, bf16[1024,128]{1,0:T(8,128)(2,1)S(1)} %copy.167.q_ref, bf16[2,1024,128]{2,1,0:T(8,128)(2,1)S(1)} %copy-done.2, s32[1024,1]{1,0:T(8,128)S(1)} %copy.168.begin_ref, bf16[1024,128]{1,0:T(8,128)(2,1)S(1)} %get-tuple-element.92.g_ref, ...), custom_call_target="tpu_custom_call" | custom-call | flops 8589934592 | bytes 8388608 | tf_op jit(solution)/shard_map/attend_back/pallas_call | solution.py:308
  282.2 9.1 %across_6.1 = bf16[2,1024,128]{2,1,0:T(8,128)(2,1)} custom-call(bf16[2,1024,128]{2,1,0:T(8,128)(2,1)} %copy-done.3), custom_call_target="tpu_custom_call" | custom-call | tf_op jit(solution)/shard_map/across_6/pallas_call | solution.py:136
  297.2 2.2 fusion.14
  300.8 3.1 convolution_convert_fusion.5
  307.7 16.9 %across_9.1 = bf16[4,576,256]{2,1,0:T(8,128)(2,1)} custom-call(bf16[4,576,256]{2,1,0:T(8,128)(2,1)} %copy.191.x_ref), custom_call_target="tpu_custom_call" | custom-call | tf_op jit(solution)/shard_map/across_9/pallas_call | solution.py:136
  327.2 2.9 collective-permute-start.5
  330.1 4.7 collective-permute-start.7
  335.0 6.8 %reshape.419 = bf16[2,2,288,2,512]{4,3,2,1,0:T(2,128)(2,1)} reshape(bf16[1152,1024]{1,0:T(8,128)(2,1)} %convolution_convert_fusion) | data formatting | bytes 4718592 | tf_op jit(solution)/shard_map/reshape | solution.py:495
  341.8 3.5 copy.188
  345.3 36.4 %across_8.1 = bf16[4,2,288,512]{3,2,1,0:T(8,128)(2,1)} custom-call(bf16[4,2,288,512]{3,2,1,0:T(8,128)(2,1)} %bitcast.149), custom_call_target="tpu_custom_call" | custom-call | tf_op jit(solution)/shard_map/across_8/pallas_call | solution.py:136
  381.7 2.1 convert_reduce_fusion
  385.0 4.4 reshape_reshape.3
  392.4 9.4 %across_11.1 = bf16[4,512,64]{2,1,0:T(8,128)(2,1)} custom-call(bf16[4,512,64]{2,1,0:T(8,128)(2,1)} %bitcast.169), custom_call_target="tpu_custom_call" | custom-call | tf_op jit(solution)/shard_map/across_11/pallas_call | solution.py:136
  406.4 9.5 %across_12.1 = bf16[4,512,128]{2,1,0:T(8,128)(2,1)} custom-call(bf16[4,512,128]{2,1,0:T(8,128)(2,1)} %bitcast.170), custom_call_target="tpu_custom_call" | custom-call | tf_op jit(solution)/shard_map/across_12/pallas_call | solution.py:136
  417.8 3.3 convolution_convert_fusion.2
  421.2 27.5 %scatter8_7.1 = f32[128,1024]{1,0:T(8,128)} custom-call(bf16[8,128,1024]{2,1,0:T(8,128)(2,1)} %bitcast.163), custom_call_target="tpu_custom_call" | custom-call | tf_op jit(solution)/shard_map/scatter8_7/pallas_call | solution.py:188
  450.6 11.8 %gather8_13.1 = f32[8,17,128]{2,1,0:T(8,128)} custom-call(f32[17,128]{1,0:T(8,128)} %bitcast.178), custom_call_target="tpu_custom_call" | custom-call | tf_op jit(solution)/shard_map/gather8_13/pallas_call | solution.py:92
  464.0 5.0 %across_14.1 = f32[4,17,128]{2,1,0:T(8,128)} custom-call(f32[17,128]{1,0:T(8,128)} %reduce_sum.246.x_ref), custom_call_target="tpu_custom_call" | custom-call | tf_op jit(solution)/shard_map/across_14/pallas_call | solution.py:136
  470.4 2.4 fusion.20
  476.8 2.7 reshape.430
  (238 shorter events, 55.3 us)
Async XLA Ops:
  3.5 76.4 %copy-start.22 = (bf16[512,64]{1,0:T(8,128)(2,1)}, bf16[512,64]{1,0:T(8,128)(2,1)S(1)}, u32[]{:S(2)}) copy-start(bf16[512,64]{1,0:T(8,128)(2,1)S(1)} %get-tuple-element.117) | copy-start | bytes 196612
  3.7 76.3 %collective-permute-start = (bf16[512,256]{1,0:T(8,128)(2,1)S(1)}, bf16[512,256]{1,0:T(8,128)(2,1)}, u32[]{:S(2)}, u32[]{:S(2)}) collective-permute-start(bf16[512,256]{1,0:T(8,128)(2,1)S(1)} %pad_maximum_fusion.8), channel_id=1, source_target_pairs={{0,1},{1,0},{2,3},{3,2},{4,5},{5,4},{6,7},{7,6},{8,9},{9,8},{10,11... | collective-permute-start | bytes 786440 | tf_op jit(solution)/shard_map/ppermute | solution.py:403
  39.7 8.2 %copy-start.9 = (bf16[1,128,1024]{2,1,0:T(8,128)(2,1)S(1)}, bf16[1,128,1024]{2,1,0:T(8,128)(2,1)}, u32[]{:S(2)}) copy-start(bf16[1,128,1024]{2,1,0:T(8,128)(2,1)} %param.14) | copy-start | bytes 786436
  45.3 5.4 %copy-start.61 = (s32[1,8]{1,0:T(1,128)S(1)}, s32[1,8]{1,0:T(1,128)}, u32[]{:S(2)}) copy-start(s32[1,8]{1,0:T(1,128)} %param.15) | copy-start | bytes 100
  45.3 95.0 %collective-permute-start.1 = (bf16[512,1024]{1,0:T(8,128)(2,1)}, bf16[512,1024]{1,0:T(8,128)(2,1)}, u32[]{:S(2)}, u32[]{:S(2)}) collective-permute-start(bf16[512,1024]{1,0:T(8,128)(2,1)} %convert_element_type.105), channel_id=1, source_target_pairs={{0,1},{1,0},{2,3},{3,2},{4,5},{5,4},{6,7},{7,6},{8,9},{9,8},{10,11... | collective-permute-start | bytes 3145736 | tf_op jit(solution)/shard_map/ppermute | solution.py:403
  45.8 103.3 %collective-permute-start.3 = (bf16[512,1152]{1,0:T(8,128)(2,1)}, bf16[512,1152]{1,0:T(8,128)(2,1)}, u32[]{:S(2)}, u32[]{:S(2)}) collective-permute-start(bf16[512,1152]{1,0:T(8,128)(2,1)} %concatenate.54), channel_id=1, source_target_pairs={{0,1},{1,0},{2,3},{3,2},{4,5},{5,4},{6,7},{7,6},{8,9},{9,8},{10,11... | collective-permute-start | bytes 3538952 | tf_op jit(solution)/shard_map/ppermute | solution.py:403
  47.4 108.5 %collective-permute-start.2 = (bf16[576,1024]{1,0:T(8,128)(2,1)}, bf16[576,1024]{1,0:T(8,128)(2,1)}, u32[]{:S(2)}, u32[]{:S(2)}) collective-permute-start(bf16[576,1024]{1,0:T(8,128)(2,1)} %pad_maximum_fusion.4), channel_id=1, source_target_pairs={{0,1},{1,0},{2,3},{3,2},{4,5},{5,4},{6,7},{7,6},{8,9},{9,8},{10,11... | collective-permute-start | bytes 3538952 | tf_op jit(solution)/shard_map/ppermute | solution.py:403
  50.5 29.5 %copy-start.25 = (bf16[512,64]{1,0:T(8,128)(2,1)S(1)}, bf16[512,64]{1,0:T(8,128)(2,1)}, u32[]{:S(2)}) copy-start(bf16[512,64]{1,0:T(8,128)(2,1)} %copy-done.24) | copy-start | bytes 196612
  50.5 29.5 %copy-start.32 = (bf16[512,128]{1,0:T(8,128)(2,1)S(1)}, bf16[512,128]{1,0:T(8,128)(2,1)}, u32[]{:S(2)}) copy-start(bf16[512,128]{1,0:T(8,128)(2,1)} %copy-done.31) | copy-start | bytes 393220
  50.5 29.5 %copy-start.39 = (f32[1024]{0:T(1024)S(1)}, f32[1024]{0:T(1024)}, u32[]{:S(2)}) copy-start(f32[1024]{0:T(1024)} %param.16) | copy-start | bytes 12292
  50.6 32.7 %copy-start.45 = (f32[1024]{0:T(1024)}, f32[1024]{0:T(1024)S(1)}, u32[]{:S(2)}) copy-start(f32[1024]{0:T(1024)S(1)} %add_rsqrt_fusion.1) | copy-start | bytes 12292
  51.0 33.7 %copy-start.35 = (f32[1024]{0:T(1024)}, f32[1024]{0:T(1024)S(1)}, u32[]{:S(2)}) copy-start(f32[1024]{0:T(1024)S(1)} %subtract_convert_fusion) | copy-start | bytes 12292
  51.6 31.7 %copy-start.51 = (f32[32]{0:T(128)}, f32[32]{0:T(128)S(1)}, u32[]{:S(2)}) copy-start(f32[32]{0:T(128)S(1)} %multiply_power_fusion) | copy-start | bytes 388
  83.3 14.8 %copy-start.6 = (f32[1024,256]{0,1:T(8,128)}, f32[1024,256]{0,1:T(8,128)S(1)}, u32[]{:S(2)}) copy-start(f32[1024,256]{0,1:T(8,128)S(1)} %fusion.46) | copy-start | bytes 3145732
  84.5 4.5 copy-start.37
  143.8 5.2 %copy-start.16 = (bf16[1024,1024]{1,0:T(8,128)(2,1)}, bf16[1024,1024]{1,0:T(8,128)(2,1)S(1)}, u32[]{:S(2)}) copy-start(bf16[1024,1024]{1,0:T(8,128)(2,1)S(1)} %maximum_select_fusion.1) | copy-start | bytes 6291460
  143.8 5.3 %copy-start.41 = (f32[1024]{0:T(1024)S(1)}, f32[1024]{0:T(1024)}, u32[]{:S(2)}) copy-start(f32[1024]{0:T(1024)} %param.19) | copy-start | bytes 12292
  148.9 12.9 %copy-start.20 = (f32[1024,1024]{1,0:T(8,128)}, f32[1024,1024]{1,0:T(8,128)S(1)}, u32[]{:S(2)}) copy-start(f32[1024,1024]{1,0:T(8,128)S(1)} %get-tuple-element.116) | copy-start | bytes 12582916
  149.1 75.6 %copy-start.49 = (f32[128]{0:T(128)}, f32[128]{0:T(128)S(1)}, u32[]{:S(2)}) copy-start(f32[128]{0:T(128)S(1)} %fusion.38) | copy-start | bytes 1540
  149.1 6.8 %copy-start.15 = (bf16[8,128,1024]{2,1,0:T(8,128)(2,1)S(1)}, bf16[8,128,1024]{2,1,0:T(8,128)(2,1)}, u32[]{:S(2)}) copy-start(bf16[8,128,1024]{2,1,0:T(8,128)(2,1)} %gather8_15.1) | copy-start | bytes 6291460
  177.1 47.6 %copy-start.11 = (bf16[1,128,1024]{2,1,0:T(8,128)(2,1)S(1)}, bf16[1,128,1024]{2,1,0:T(8,128)(2,1)}, u32[]{:S(2)}) copy-start(bf16[1,128,1024]{2,1,0:T(8,128)(2,1)} %param.27) | copy-start | bytes 786436
  224.6 40.1 %copy-start.55 = (f32[128]{0:T(128)}, f32[128]{0:T(128)S(1)}, u32[]{:S(2)}) copy-start(f32[128]{0:T(128)S(1)} %multiply_multiply_fusion.4) | copy-start | bytes 1540
  300.8 4.6 copy-start.17
  327.2 146.2 %collective-permute-start.5 = (f32[576,64]{0,1:T(8,128)}, f32[576,64]{0,1:T(8,128)}, u32[]{:S(2)}, u32[]{:S(2)}) collective-permute-start(f32[576,64]{0,1:T(8,128)} %get-tuple-element.97), channel_id=1, source_target_pairs={{0,0},{1,16},{2,2},{3,18},{4,4},{5,20},{6,6},{7,22},{8,8},{9,24},{... | collective-permute-start | bytes 442376 | tf_op jit(solution)/shard_map/ppermute | solution.py:525
  330.1 143.3 %collective-permute-start.6 = (f32[576,64]{0,1:T(8,128)}, f32[576,64]{0,1:T(8,128)}, u32[]{:S(2)}, u32[]{:S(2)}) collective-permute-start(f32[576,64]{0,1:T(8,128)} %get-tuple-element.100), channel_id=1, source_target_pairs={{0,2},{1,18},{2,0},{3,16},{4,6},{5,22},{6,4},{7,20},{8,10},{9,26},... | collective-permute-start | bytes 442376 | tf_op jit(solution)/shard_map/ppermute | solution.py:525
  330.1 143.3 %collective-permute-start.7 = (f32[576,64]{0,1:T(8,128)}, f32[576,64]{0,1:T(8,128)}, u32[]{:S(2)}, u32[]{:S(2)}) collective-permute-start(f32[576,64]{0,1:T(8,128)} %get-tuple-element.99), channel_id=1, source_target_pairs={{0,8},{1,24},{2,10},{3,26},{4,12},{5,28},{6,14},{7,30},{8,0},{9,16... | collective-permute-start | bytes 442376 | tf_op jit(solution)/shard_map/ppermute | solution.py:525
  334.9 138.6 %collective-permute-start.8 = (f32[576,64]{0,1:T(8,128)S(1)}, f32[576,64]{0,1:T(8,128)}, u32[]{:S(2)}, u32[]{:S(2)}) collective-permute-start(f32[576,64]{0,1:T(8,128)S(1)} %get-tuple-element.98), channel_id=1, source_target_pairs={{0,10},{1,26},{2,8},{3,24},{4,14},{5,30},{6,12},{7,28},{8,2},{9,18... | collective-permute-start | bytes 442376 | tf_op jit(solution)/shard_map/ppermute | solution.py:525
  385.0 5.3 %copy-start.8 = (bf16[1024,8,128]{0,2,1:T(8,128)(2,1)S(1)}, bf16[1024,8,128]{0,2,1:T(8,128)(2,1)}, u32[]{:S(2)}) copy-start(bf16[1024,8,128]{0,2,1:T(8,128)(2,1)} %copy.169) | copy-start | bytes 6291460
  391.0 12.8 %slice-start.1 = ((bf16[1024,256]{0,1:T(8,128)(2,1)}), bf16[1024,128]{0,1:T(8,128)(2,1)S(1)}, s32[]{:S(2)}) async-start(bf16[1024,256]{0,1:T(8,128)(2,1)} %copy-done.13), calls=%async_computation.1 | async-start | bytes 524288 | tf_op jit(solution)/shard_map/slice | solution.py:546
  391.2 13.1 %copy-start.34 = (bf16[1024,64]{0,1:T(8,128)(2,1)S(1)}, bf16[1024,64]{0,1:T(8,128)(2,1)}, u32[]{:S(2)}) copy-start(bf16[1024,64]{0,1:T(8,128)(2,1)} %get-tuple-element.105) | copy-start | bytes 393220
  404.8 13.0 %copy-start.19 = (bf16[1024,2,64]{0,2,1:T(8,128)(2,1)S(1)}, bf16[1024,2,64]{0,2,1:T(8,128)(2,1)}, u32[]{:S(2)}) copy-start(bf16[1024,2,64]{0,2,1:T(8,128)(2,1)} %copy-done.18) | copy-start | bytes 786436
  404.8 13.0 %copy-start.23 = (bf16[512,64]{1,0:T(8,128)(2,1)S(1)}, bf16[512,64]{1,0:T(8,128)(2,1)}, u32[]{:S(2)}) copy-start(bf16[512,64]{1,0:T(8,128)(2,1)} %copy-done.22) | copy-start | bytes 196612
  404.8 13.0 %copy-start.26 = (bf16[512,64]{1,0:T(8,128)(2,1)S(1)}, bf16[512,64]{1,0:T(8,128)(2,1)}, u32[]{:S(2)}) copy-start(bf16[512,64]{1,0:T(8,128)(2,1)} %copy-done.24) | copy-start | bytes 196612
  404.8 13.0 %copy-start.28 = (bf16[1024,64]{0,1:T(8,128)(2,1)S(1)}, bf16[1024,64]{0,1:T(8,128)(2,1)}, u32[]{:S(2)}) copy-start(bf16[1024,64]{0,1:T(8,128)(2,1)} %copy-done.27) | copy-start | bytes 393220
  404.8 13.0 %copy-start.30 = (bf16[1024,64]{0,1:T(8,128)(2,1)S(1)}, bf16[1024,64]{0,1:T(8,128)(2,1)}, u32[]{:S(2)}) copy-start(bf16[1024,64]{0,1:T(8,128)(2,1)} %copy-done.29) | copy-start | bytes 393220
  404.8 13.0 %copy-start.33 = (bf16[512,128]{1,0:T(8,128)(2,1)S(1)}, bf16[512,128]{1,0:T(8,128)(2,1)}, u32[]{:S(2)}) copy-start(bf16[512,128]{1,0:T(8,128)(2,1)} %copy-done.31) | copy-start | bytes 393220
  417.1 62.5 %collective-permute-start.4 = (f32[512,128]{1,0:T(8,128)S(1)}, f32[512,128]{1,0:T(8,128)S(1)}, u32[]{:S(2)}, u32[]{:S(2)}) collective-permute-start(f32[512,128]{1,0:T(8,128)S(1)} %convert_reduce_fusion.3), channel_id=1, source_target_pairs={{0,0},{1,1},{2,4},{3,5},{4,2},{5,3},{6,6},{7,7},{8,8},{9,9},{10,12... | collective-permute-start | bytes 786440 | tf_op jit(solution)/shard_map/ppermute | solution.py:558
  421.1 27.6 %copy-start.10 = (bf16[1,128,1024]{2,1,0:T(8,128)(2,1)S(1)}, bf16[1,128,1024]{2,1,0:T(8,128)(2,1)}, u32[]{:S(2)}) copy-start(bf16[1,128,1024]{2,1,0:T(8,128)(2,1)} %param.14) | copy-start | bytes 786436
  421.1 27.6 %copy-start.57 = (f32[128]{0:T(128)S(1)}, f32[128]{0:T(128)}, u32[]{:S(2)}) copy-start(f32[128]{0:T(128)} %fusion.39) | copy-start | bytes 1540
  421.1 28.8 %copy-start.47 = (f32[1024]{0:T(1024)S(1)}, f32[1024]{0:T(1024)}, u32[]{:S(2)}) copy-start(f32[1024]{0:T(1024)} %get-tuple-element.70) | copy-start | bytes 12292
  421.1 28.8 %copy-start.58 = (f32[64]{0:T(128)S(1)}, f32[64]{0:T(128)}, u32[]{:S(2)}) copy-start(f32[64]{0:T(128)} %get-tuple-element.76) | copy-start | bytes 772
  421.1 49.2 %copy-start.60 = (f32[128]{0:T(128)S(1)}, f32[128]{0:T(128)}, u32[]{:S(2)}) copy-start(f32[128]{0:T(128)} %copy-done.59) | copy-start | bytes 1540
  421.1 49.2 %copy-start.5 = (f32[2,128,1024]{2,1,0:T(8,128)S(1)}, f32[2,128,1024]{2,1,0:T(8,128)}, u32[]{:S(2)}) copy-start(f32[2,128,1024]{2,1,0:T(8,128)} %scatter8_4.1) | copy-start | bytes 3145732
  421.1 49.2 %copy-start.12 = (bf16[1,128,1024]{2,1,0:T(8,128)(2,1)S(1)}, bf16[1,128,1024]{2,1,0:T(8,128)(2,1)}, u32[]{:S(2)}) copy-start(bf16[1,128,1024]{2,1,0:T(8,128)(2,1)} %param.27) | copy-start | bytes 786436
  421.1 49.2 %copy-start.42 = (f32[1024]{0:T(1024)S(1)}, f32[1024]{0:T(1024)}, u32[]{:S(2)}) copy-start(f32[1024]{0:T(1024)} %param.19) | copy-start | bytes 12292
  421.2 49.2 %copy-start.50 = (f32[128]{0:T(128)S(1)}, f32[128]{0:T(128)}, u32[]{:S(2)}) copy-start(f32[128]{0:T(128)} %copy-done.49) | copy-start | bytes 1540
  421.2 49.2 %copy-start.56 = (f32[128]{0:T(128)S(1)}, f32[128]{0:T(128)}, u32[]{:S(2)}) copy-start(f32[128]{0:T(128)} %copy-done.55) | copy-start | bytes 1540
  475.3 6.7 %copy-start.1 = (f32[512,1024]{1,0:T(8,128)S(1)}, f32[512,1024]{1,0:T(8,128)}, u32[]{:S(2)}) copy-start(f32[512,1024]{1,0:T(8,128)} %param.20) | copy-start | bytes 6291460
  (25 other events, 60.1 us)
